TPU v7x, 32 devices: a whole 2x2x4 slice. The times are simulated.
32 devices in a mesh: row: 16 (over z, y, x), wt: 2 (over core).
Axes of the slice: x: 2, y: 2, z: 4, core: 2. Of those that a mesh axis runs over, the one named last changes fastest.
Arguments:
- atoms: bfloat16 [2, 2048, 768], P('wt', 'row'), may hold values from -6 to 6
- coords: bfloat16 [3, 2, 2048], P(None, 'wt', 'row'), may hold values from -8 to 8
- atom_types: int32 [2, 2048], P('wt', 'row'), may hold values from 0 to 127
- lengths: int32 [2, 16], P('wt'), may hold values from 1 to 1024, 2048 in all within a row
- times: float32 [2], P('wt'), may hold values from 0.05 to 1
- type_table: bfloat16 [128, 768], replicated, may hold values from -3 to 3
- gain_one: float32 [768], replicated, may hold values from 0.5 to 1.5
- shift_one: float32 [768], replicated, may hold values from -1 to 1
- w_qkv: bfloat16 [768, 2304], P('wt'), may hold values from -0.21875 to 0.21875
- centers: float32 [128], replicated, may hold values from 0 to 12
- widths: float32 [128], replicated, may hold values from 0.05 to 120
- w_pair: bfloat16 [128, 32], replicated, may hold values from -460 to 460
- w_out: bfloat16 [768, 768], P('wt'), may hold values from -0.875 to 0.875
- gain_two: float32 [768], replicated, may hold values from 0.5 to 1.5
- shift_two: float32 [768], replicated, may hold values from -1 to 1
- w_up: bfloat16 [768, 3072], P('wt'), may hold values from -0.21875 to 0.21875
- w_down: bfloat16 [3072, 768], P('wt'), may hold values from -0.109375 to 0.109375
- w_force: bfloat16 [3, 768], replicated, may hold values from -0.21875 to 0.21875
- out_grad: bfloat16 [2, 2048, 768], P('wt', 'row'), may hold values from -6 to 6
- force_grad: float32 [3, 2, 2048], P(None, 'wt', 'row'), may hold values from -6 to 6
Outputs:
- block_out: bfloat16 [2, 2048, 768], P('wt', 'row')
- forces: float32 [3, 2, 2048], P(None, 'wt', 'row')
- atoms_grad: float32 [2, 2048, 768], P('wt', 'row')
- type_table_grad: float32 [128, 768], replicated
- gain_one_grad: float32 [768], replicated
- shift_one_grad: float32 [768], replicated
- w_qkv_grad: float32 [768, 2304], P('wt', 'row')
- centers_grad: float32 [128], replicated
- widths_grad: float32 [128], replicated
- w_pair_grad: float32 [128, 32], replicated
- w_out_grad: float32 [768, 768], P('wt', 'row')
- gain_two_grad: float32 [768], replicated
- shift_two_grad: float32 [768], replicated
- w_up_grad: float32 [768, 3072], P('wt', 'row')
- w_down_grad: float32 [3072, 768], P('wt', 'row')
- w_force_grad: float32 [3, 768], replicated
Inputs may be any that keep to these rules, and one draw needn't show every extreme that they name: Each micro-batch's molecules fill its 2048 positions in order, their lengths summing to 2048; some molecule has exactly 1024 atoms.
All inputs are finite; a program needn't handle non-finite values.
Results may differ from a plain program's by a relative error of at most 0.019.
Values may be sent and summed in bfloat16 or wider, within the bound.
A program may use at most 192 MiB of HBM per device.

v0:
```python
import math

import jax
import jax.numpy as jnp
from jax import lax
from jax.sharding import PartitionSpec as P

MAXLEN = 1024


NEG_FILL = -1e30
HIGHEST = lax.Precision.HIGHEST


def shifted(x, axis, by):
    length = lax.axis_size(axis)
    pairs = [(i, i + by) for i in range(length) if 0 <= i + by < length]
    return lax.ppermute(x, axis, pairs)


def norm_parts(values_in):
    average = jnp.mean(values_in, axis=-1, keepdims=True)
    centred = values_in - average
    inverse = lax.rsqrt(jnp.mean(centred * centred, axis=-1, keepdims=True) + 1e-05)
    return (centred * inverse, inverse)


def norm_back(grad_out, normed, inverse, gain_vec):
    grad_normed = grad_out * gain_vec
    mean_grad = jnp.mean(grad_normed, axis=-1, keepdims=True)
    mean_mixed = jnp.mean(grad_normed * normed, axis=-1, keepdims=True)
    grad_in = inverse * (grad_normed - mean_grad - normed * mean_mixed)
    return (grad_in, jnp.sum(grad_out * normed, axis=0), jnp.sum(grad_out, axis=0))


def gelu_tanh(values_in):
    return (
        0.5
        * values_in
        * (
            1.0
            + jnp.tanh(
                0.7978845608028654 * (values_in + 0.044715 * values_in * values_in * values_in)
            )
        )
    )


def time_code(moment, model_width):
    half_width = model_width // 2
    frequency = jnp.exp(-math.log(10000.0) * jnp.arange(half_width, dtype=jnp.float32) / half_width)
    angles = 100.0 * moment * frequency
    return jnp.concatenate([jnp.sin(angles), jnp.cos(angles)])


def item_ids(places, item_ends):
    return jnp.sum((places[:, None] >= item_ends[None, :]).astype(jnp.int32), axis=1)


def kernel_terms(query_pos, key_pos, centers, widths):
    differ = query_pos[:, :, None] - key_pos[:, None, :]
    distance = jnp.sqrt(jnp.sum(differ * differ, axis=0))
    scaled_gap = (distance[:, :, None] - centers) / widths
    return (
        scaled_gap,
        jnp.exp(-0.5 * scaled_gap * scaled_gap) / (math.sqrt(2.0 * math.pi) * widths),
    )


def cross_rows(left_side, right_side):
    return lax.dot_general(
        left_side, right_side, (((0,), (0,)), ((), ())), preferred_element_type=jnp.float32
    )


def along_rows(left_side, right_side):
    return lax.dot_general(
        left_side, right_side, (((1,), (1,)), ((), ())), preferred_element_type=jnp.float32
    )


def on_device(
    atoms,
    coords,
    atom_types,
    lengths,
    times,
    type_table,
    gain_one,
    shift_one,
    w_qkv,
    centers,
    widths,
    w_pair,
    w_out,
    gain_two,
    shift_two,
    w_up,
    w_down,
    w_force,
    out_grad,
    force_grad,
):
    micro_count, row_count, model_width = atoms.shape
    head_count = w_pair.shape[1]
    head_dim = model_width // head_count
    score_scale = head_dim ** (-0.5)
    my_index = lax.axis_index("row")
    reach_shards = (MAXLEN - 2) // row_count + 1
    span_shards = 2 * reach_shards + 1
    all_rows = row_count * lax.axis_size("row")
    type_codes = jnp.arange(type_table.shape[0], dtype=jnp.int32)
    plan_steps = []
    have_count = 1
    while have_count < reach_shards + 1:
        take_count = min(have_count, reach_shards + 1 - have_count)
        plan_steps.append((have_count, take_count))
        have_count = have_count + take_count
    block_outs, force_rows, atom_grads = ([], [], [])
    w_qkv_full = lax.all_gather(w_qkv, "wt", axis=0, tiled=True)
    w_out_full = lax.all_gather(w_out, "wt", axis=0, tiled=True)
    w_up_full = lax.all_gather(w_up, "wt", axis=0, tiled=True)
    w_down_full = lax.all_gather(w_down, "wt", axis=0, tiled=True)
    item_ends = jnp.cumsum(lengths[0])
    own_ids = item_ids(my_index * row_count + jnp.arange(row_count, dtype=jnp.int32), item_ends)
    onehot = (atom_types[0][:, None] == type_codes[None, :]).astype(jnp.bfloat16)
    base_rows = (
        atoms[0].astype(jnp.float32)
        + time_code(times[0], model_width)
        + jnp.dot(onehot, type_table, preferred_element_type=jnp.float32)
    )
    normed_one, inverse_one = norm_parts(base_rows)
    normed_in = (normed_one * gain_one + shift_one).astype(jnp.bfloat16)
    qkv_rows = jnp.dot(normed_in, w_qkv_full, preferred_element_type=jnp.float32).astype(
        jnp.bfloat16
    )
    queries = qkv_rows[:, :model_width].reshape(row_count, head_count, head_dim)
    own_keys = (
        qkv_rows[:, model_width : 2 * model_width],
        qkv_rows[:, 2 * model_width :],
        coords[:, 0, :],
    )
    query_pos = coords[:, 0, :].astype(jnp.float32)
    fetched = {}
    for offset in range(1, reach_shards + 1):
        for direction in (1, -1):
            fetched[direction * offset] = shifted(
                (own_keys[0], own_keys[1], own_keys[2]), "row", direction * offset
            )
    ordered = (
        [fetched[offset] for offset in range(reach_shards, 0, -1)]
        + [own_keys]
        + [fetched[-offset] for offset in range(1, reach_shards + 1)]
    )
    key_rows = jnp.concatenate([member[0] for member in ordered], axis=0)
    value_rows = jnp.concatenate([member[1] for member in ordered], axis=0)
    key_pos = jnp.concatenate([member[2] for member in ordered], axis=1)
    key_places = (my_index - reach_shards) * row_count + jnp.arange(
        span_shards * row_count, dtype=jnp.int32
    )
    inside = (key_places >= 0) & (key_places < all_rows)
    key_items = jnp.where(inside, item_ids(key_places, item_ends), -1)
    shards_in = (
        key_rows.reshape(span_shards, row_count, model_width),
        value_rows.reshape(span_shards, row_count, model_width),
        jnp.transpose(key_pos.reshape(3, span_shards, row_count), (1, 0, 2)),
        key_items.reshape(span_shards, row_count),
    )

    def shard_logits(shard_keys, shard_pos, shard_items):
        scaled_gap, kernel = kernel_terms(query_pos, shard_pos.astype(jnp.float32), centers, widths)
        kernel_low = kernel.astype(jnp.bfloat16)
        pair_bias = jnp.einsum(
            "qkc,ch->hqk", kernel_low, w_pair, preferred_element_type=jnp.float32
        )
        scores = (
            score_scale
            * jnp.einsum(
                "qhd,khd->hqk",
                queries,
                shard_keys.reshape(row_count, head_count, head_dim),
                preferred_element_type=jnp.float32,
            )
            + pair_bias
        )
        same_item = (own_ids[:, None] == shard_items[None, :])[None, :, :]
        return (jnp.where(same_item, scores, NEG_FILL), same_item, scaled_gap, kernel, kernel_low)

    def forward_step(carry, shard):
        row_top, row_total, weighted_sum = carry
        shard_keys, shard_values, shard_pos, shard_items = shard
        logits, same_item, scaled_gap, kernel, kernel_low = shard_logits(
            shard_keys, shard_pos, shard_items
        )
        new_top = jnp.maximum(row_top, jnp.max(logits, axis=-1))
        weights = jnp.where(same_item, jnp.exp(logits - new_top[:, :, None]), 0.0)
        fading = jnp.exp(row_top - new_top)
        row_total = row_total * fading + jnp.sum(weights, axis=-1)
        values_here = shard_values.reshape(row_count, head_count, head_dim).astype(jnp.float32)
        weighted_sum = weighted_sum * jnp.transpose(fading)[:, :, None] + jnp.einsum(
            "hqk,khd->qhd",
            weights,
            values_here,
            precision=HIGHEST,
            preferred_element_type=jnp.float32,
        )
        return ((new_top, row_total, weighted_sum), None)

    start_state = (
        jnp.full((head_count, row_count), NEG_FILL, jnp.float32),
        jnp.zeros((head_count, row_count), jnp.float32),
        jnp.zeros((row_count, head_count, head_dim), jnp.float32),
    )
    (row_top, row_total, weighted_sum), _ = lax.scan(forward_step, start_state, shards_in)
    log_total = row_top + jnp.log(row_total)
    attended = (weighted_sum / jnp.transpose(row_total)[:, :, None]).reshape(row_count, model_width)
    att_low = attended.astype(jnp.bfloat16)
    after_att = base_rows + jnp.dot(att_low, w_out_full, preferred_element_type=jnp.float32)
    normed_two, inverse_two = norm_parts(after_att)
    ffn_in = (normed_two * gain_two + shift_two).astype(jnp.bfloat16)
    hidden = jnp.dot(ffn_in, w_up_full, preferred_element_type=jnp.float32)
    activated_full, gelu_pull = jax.vjp(gelu_tanh, hidden)
    activated = activated_full.astype(jnp.bfloat16)
    block_sum = after_att + jnp.dot(activated, w_down_full, preferred_element_type=jnp.float32)
    out_low = block_sum.astype(jnp.bfloat16)
    block_outs.append(out_low)
    force_rows.append(along_rows(w_force, out_low))
    force_cot = force_grad[:, 0, :]
    grad_sum = out_grad[0].astype(jnp.float32) + lax.dot_general(
        force_cot,
        w_force.astype(jnp.float32),
        (((0,), (0,)), ((), ())),
        precision=HIGHEST,
        preferred_element_type=jnp.float32,
    )
    grad_force = jnp.dot(
        force_cot,
        out_low.astype(jnp.float32),
        precision=HIGHEST,
        preferred_element_type=jnp.float32,
    )
    grad_sum_low = grad_sum.astype(jnp.bfloat16)
    grad_down_w = cross_rows(activated, grad_sum_low)
    grad_act_low = along_rows(grad_sum_low, w_down_full).astype(jnp.bfloat16)
    grad_hidden_low = gelu_pull(grad_act_low.astype(jnp.float32))[0].astype(jnp.bfloat16)
    grad_up_w = cross_rows(ffn_in, grad_hidden_low)
    grad_ffn_in = along_rows(grad_hidden_low, w_up_full)
    grad_norm_two, gain_part, shift_part = norm_back(grad_ffn_in, normed_two, inverse_two, gain_two)
    grad_gain_two = gain_part
    grad_shift_two = shift_part
    grad_after = grad_sum + grad_norm_two
    grad_after_low = grad_after.astype(jnp.bfloat16)
    grad_out_w = cross_rows(att_low, grad_after_low)
    grad_att_low = along_rows(grad_after_low, w_out_full).astype(jnp.bfloat16)
    grad_att_heads = grad_att_low.reshape(row_count, head_count, head_dim)
    delta_rows = jnp.transpose(
        jnp.sum(
            grad_att_heads.astype(jnp.float32) * attended.reshape(row_count, head_count, head_dim),
            axis=2,
        )
    )

    def backward_step(carry, shard):
        grad_queries, pair_part, center_part, width_part = carry
        shard_keys, shard_values, shard_pos, shard_items = shard
        logits, same_item, scaled_gap, kernel, kernel_low = shard_logits(
            shard_keys, shard_pos, shard_items
        )
        weights = jnp.where(same_item, jnp.exp(logits - log_total[:, :, None]), 0.0)
        keys_here = shard_keys.reshape(row_count, head_count, head_dim)
        values_here = shard_values.reshape(row_count, head_count, head_dim)
        grad_weights = jnp.einsum(
            "qhd,khd->hqk", grad_att_heads, values_here, preferred_element_type=jnp.float32
        )
        grad_logits = (weights * (grad_weights - delta_rows[:, :, None])).astype(jnp.bfloat16)
        grad_queries = grad_queries + jnp.einsum(
            "hqk,khd->qhd", grad_logits, keys_here, preferred_element_type=jnp.float32
        )
        key_grad = (
            jnp.einsum("hqk,qhd->khd", grad_logits, queries, preferred_element_type=jnp.float32)
            * score_scale
        )
        value_grad = jnp.einsum(
            "hqk,qhd->khd",
            weights,
            grad_att_heads.astype(jnp.float32),
            precision=HIGHEST,
            preferred_element_type=jnp.float32,
        )
        pair_part = pair_part + jnp.einsum(
            "qkc,hqk->ch", kernel_low, grad_logits, preferred_element_type=jnp.float32
        )
        grad_kernel = jnp.einsum(
            "hqk,ch->qkc", grad_logits, w_pair, preferred_element_type=jnp.float32
        )
        weighted = grad_kernel * kernel
        center_part = center_part + jnp.sum(weighted * scaled_gap, axis=(0, 1)) / widths
        width_part = (
            width_part + jnp.sum(weighted * (scaled_gap * scaled_gap - 1.0), axis=(0, 1)) / widths
        )
        return (
            (grad_queries, pair_part, center_part, width_part),
            (key_grad.reshape(row_count, model_width), value_grad.reshape(row_count, model_width)),
        )

    back_state = (
        jnp.zeros((row_count, head_count, head_dim), jnp.float32),
        jnp.zeros(w_pair.shape, jnp.float32),
        jnp.zeros(centers.shape, jnp.float32),
        jnp.zeros(widths.shape, jnp.float32),
    )
    (grad_queries, pair_part, center_part, width_part), (key_grads, value_grads) = lax.scan(
        backward_step, back_state, shards_in
    )
    own_key_grad = key_grads[reach_shards]
    own_value_grad = value_grads[reach_shards]
    for offset in range(1, reach_shards + 1):
        for direction in (1, -1):
            slot_index = reach_shards - direction * offset
            arrived = (
                shifted(
                    key_grads[slot_index].astype(jnp.bfloat16), "row", -direction * offset
                ).astype(jnp.float32),
                shifted(
                    value_grads[slot_index].astype(jnp.bfloat16), "row", -direction * offset
                ).astype(jnp.float32),
            )
            own_key_grad = own_key_grad + arrived[0]
            own_value_grad = own_value_grad + arrived[1]
    qkv_grad = jnp.concatenate(
        [grad_queries.reshape(row_count, model_width) * score_scale, own_key_grad, own_value_grad],
        axis=1,
    ).astype(jnp.bfloat16)
    grad_qkv_w = cross_rows(normed_in, qkv_grad)
    grad_normed_in = along_rows(qkv_grad, w_qkv_full)
    grad_norm_one, gain_part, shift_part = norm_back(
        grad_normed_in, normed_one, inverse_one, gain_one
    )
    atoms_grad = grad_after + grad_norm_one
    atom_grads.append(atoms_grad)
    grad_table = lax.dot_general(
        onehot.astype(jnp.float32),
        atoms_grad,
        (((0,), (0,)), ((), ())),
        precision=HIGHEST,
        preferred_element_type=jnp.float32,
    )
    large_grads = (grad_qkv_w, grad_out_w, grad_up_w, grad_down_w)
    halfway = (
        lax.psum_scatter(large_grads[0], "row", scatter_dimension=1, tiled=True),
        lax.psum_scatter(large_grads[1], "row", scatter_dimension=1, tiled=True),
        lax.psum_scatter(large_grads[2], "row", scatter_dimension=1, tiled=True),
        lax.psum_scatter(large_grads[3], "row", scatter_dimension=1, tiled=True),
    )
    large_grads = (
        lax.psum_scatter(
            halfway[0].astype(jnp.bfloat16), "wt", scatter_dimension=0, tiled=True
        ).astype(jnp.float32),
        lax.psum_scatter(
            halfway[1].astype(jnp.bfloat16), "wt", scatter_dimension=0, tiled=True
        ).astype(jnp.float32),
        lax.psum_scatter(
            halfway[2].astype(jnp.bfloat16), "wt", scatter_dimension=0, tiled=True
        ).astype(jnp.float32),
        lax.psum_scatter(
            halfway[3].astype(jnp.bfloat16), "wt", scatter_dimension=0, tiled=True
        ).astype(jnp.float32),
    )
    small_sums = lax.psum(
        (
            grad_table,
            gain_part,
            shift_part,
            center_part,
            width_part,
            pair_part,
            grad_gain_two,
            grad_shift_two,
            grad_force,
        ),
        ("row", "wt"),
    )
    return (
        jnp.stack(block_outs),
        jnp.stack(force_rows, axis=1),
        jnp.stack(atom_grads),
        small_sums[0],
        small_sums[1],
        small_sums[2],
        large_grads[0],
        small_sums[3],
        small_sums[4],
        small_sums[5],
        large_grads[1],
        small_sums[6],
        small_sums[7],
        large_grads[2],
        large_grads[3],
        small_sums[8],
    )


def solution(mesh):
    in_specs = (
        P("wt", "row", None),
        P(None, "wt", "row"),
        P("wt", "row"),
        P("wt", None),
        P("wt"),
        P(),
        P(),
        P(),
        P("wt", None),
        P(),
        P(),
        P(),
        P("wt", None),
        P(),
        P(),
        P("wt", None),
        P("wt", None),
        P(),
        P("wt", "row", None),
        P(None, "wt", "row"),
    )
    out_specs = (
        P("wt", "row", None),
        P(None, "wt", "row"),
        P("wt", "row", None),
        P(),
        P(),
        P(),
        P("wt", "row"),
        P(),
        P(),
        P(),
        P("wt", "row"),
        P(),
        P(),
        P("wt", "row"),
        P("wt", "row"),
        P(),
    )
    return jax.shard_map(
        on_device, mesh=mesh, in_specs=in_specs, out_specs=out_specs, check_vma=False
    )
```

profile of v0, /device:TPU:0, one launch (start us, length us, event | category | flops | bytes accessed | tf_op | source)
XLA Modules:
  0.0 1937.7 jit_solution(2279136052108581280)
XLA Ops:
  14.8 9.7 collective-permute-start.16
  44.2 6.7 collective-permute-start.20
  83.4 7.4 collective-permute-done.26
  111.9 19.7 %collective-permute-start.1 = (bf16[128,768]{1,0:T(8,128)(2,1)S(1)}, bf16[128,768]{1,0:T(8,128)(2,1)S(1)}, u32[]{:S(2)}, u32[]{:S(2)}) collective-permute-start(bf16[128,768]{1,0:T(8,128)(2,1)S(1)} %get-tuple-element.789), channel_id=1, source_target_pairs={{0,14},{2,16},{4,18},{6,20},{8,22},{10,24},{12,26},{14,28},{16,30}... | collective-permute-start | bytes 589832 | tf_op jit(solution)/shard_map/ppermute | solution.py:18
  156.3 12.7 collective-permute-start.33
  172.2 7.3 collective-permute-start.35
  214.3 13.2 collective-permute-done.42
  231.5 13.0 collective-permute-done.44
  272.1 8.6 collective-permute-done.12
  289.0 260.0 %while.38 = (s32[]{:T(128)}, f32[32,128]{1,0:T(8,128)S(1)}, f32[32,128]{1,0:T(8,128)S(1)}, f32[128,32,24]{0,2,1:T(8,128)S(1)}, s32[128]{0:T(128)}, /*index=5*/s3...) while((s32[]{:T(128)}, f32[32,128]{1,0:T(8,128)S(1)}, ...), condition=%wide.region_9.10_spmd.clone, body=%wide.region_5.9_spmd.clone.sunk | while | flops 328147456 | bytes 17450932 | solution.py:214
  567.5 543.7 %while.39 = (s32[]{:T(128)}, f32[128,32,24]{0,2,1:T(8,128)S(1)}, f32[128,32]{0,1:T(8,128)}, f32[128]{0:T(128)}, f32[128]{0:T(128)}, /*index=5*/f32[17,128,768]{1...) while((s32[]{:T(128)}, f32[128,32,24]{0,2,1:T(8,128)S(1)}, ...), condition=%wide.region_19.20_spmd.clone, body=%wide.region_15.19_spmd.clone.sunk | while | flops 709288960 | bytes 28063464 | solution.py:312
  588.2 6.4 multiply_reduce_fusion.18
  620.3 6.4 multiply_reduce_fusion.18
  652.3 6.4 multiply_reduce_fusion.18
  684.3 6.4 multiply_reduce_fusion.18
  748.2 6.4 multiply_reduce_fusion.18
  780.2 6.4 multiply_reduce_fusion.18
  844.1 6.4 multiply_reduce_fusion.18
  876.1 6.4 multiply_reduce_fusion.18
  940.0 6.4 multiply_reduce_fusion.18
  1004.0 6.4 multiply_reduce_fusion.18
  1036.0 6.4 multiply_reduce_fusion.18
  1067.9 6.4 multiply_reduce_fusion.18
  1116.4 12.9 collective-permute-start.79
  1153.4 6.8 collective-permute-start.69
  1173.9 14.0 collective-permute-start.63
  1205.6 6.9 collective-permute-start.55
  1256.5 141.6 %reduce-scatter.15.cloned.1.call-done = f32[768,144]{0,1:T(8,128)} async-done(((f32[768,2304]{0,1:T(8,128)}), f32[768,144]{0,1:T(8,128)}) %reduce-scatter.15.cloned.1.call-update) | async-done | bytes 442384 | tf_op jit(solution)/shard_map/reduce_scatter | solution.py:350
  1403.5 170.9 %reduce-scatter.19.cloned.1.call-done = f32[768,192]{0,1:T(8,128)} async-done(((f32[768,3072]{0,1:T(8,128)}), f32[768,192]{0,1:T(8,128)}) %reduce-scatter.19.cloned.1.call-update) | async-done | bytes 589840 | tf_op jit(solution)/shard_map/reduce_scatter | solution.py:352
  1580.8 169.3 %reduce-scatter.21.cloned.1.call-done = f32[3072,48]{0,1:T(8,128)} async-done(((f32[3072,768]{0,1:T(8,128)}), f32[3072,48]{0,1:T(8,128)}) %reduce-scatter.21.cloned.1.call-update) | async-done | bytes 589840 | tf_op jit(solution)/shard_map/reduce_scatter | solution.py:353
  1753.8 40.6 %all-reduce = (f32[768]{0:T(1024)}, f32[768]{0:T(1024)}, f32[128]{0:T(128)}, f32[128]{0:T(128)}, f32[128,32]{0,1:T(8,128)}, /*index=5*/f32[768]{0:T(1024)}, f32[768]{0:T(1024)}, f32[3,768]{1,0:T(4,128)}) all-reduce(f32[768]{0:T(1024)S(1)} %get-tuple-element.661, ...), channel_id=1, replica_groups=mesh['row'=16,'wt'=2] {'row','wt'}, use_global_device_ids=true, to_apply=%region_24.25 | all-reduce | flops 9728 | bytes 77824 | tf_op jit(solution)/shard_map/psum | solution.py:369
  1801.2 127.7 %all-reduce.3.cloned.1.call-done = f32[128,768]{1,0:T(8,128)} async-done(((f32[128,768]{1,0:T(8,128)}), f32[128,768]{1,0:T(8,128)}) %all-reduce.3.cloned.1.call-update) | async-done | bytes 393232 | tf_op jit(solution)/shard_map/psum | solution.py:369
  (1317 shorter events, 1049.7 us)
Async XLA Ops:
  7.2 87.8 %all-gather.5.cloned.1.call-start = ((), (), s32[]{:S(2)}) async-start(), calls=%async_computation.8 | async-start | bytes 5308416 | tf_op jit(solution)/shard_map/all_gather | solution.py:120
  8.0 541.1 %all-gather.7.cloned.1.call-start = ((), (), s32[]{:S(2)}) async-start(), calls=%async_computation.9 | async-start | bytes 1769472 | tf_op jit(solution)/shard_map/all_gather | solution.py:121
  8.8 542.4 %all-gather.9.cloned.1.call-start = ((), (), s32[]{:S(2)}) async-start(), calls=%async_computation.10 | async-start | bytes 7077888 | tf_op jit(solution)/shard_map/all_gather | solution.py:122
  9.5 544.9 %all-gather.11.cloned.1.call-start = ((), (), s32[]{:S(2)}) async-start(), calls=%async_computation.11 | async-start | bytes 7077888 | tf_op jit(solution)/shard_map/all_gather | solution.py:123
  9.6 84.9 %collective-permute-start.30 = (bf16[3,128]{1,0:T(4,128)(2,1)S(1)}, bf16[3,128]{1,0:T(4,128)(2,1)S(1)}, u32[]{:S(2)}, u32[]{:S(2)}) collective-permute-start(bf16[3,128]{1,0:T(4,128)(2,1)S(1)} %bitcast.396), channel_id=1, source_target_pairs={{14,0},{16,2},{18,4},{20,6},{22,8},{24,10},{26,12},{28,14},{30,16}... | collective-permute-start | bytes 2312 | tf_op jit(solution)/shard_map/ppermute | solution.py:18
  10.9 83.0 %collective-permute-start.29 = (bf16[3,128]{1,0:T(4,128)(2,1)S(1)}, bf16[3,128]{1,0:T(4,128)(2,1)S(1)}, u32[]{:S(2)}, u32[]{:S(2)}) collective-permute-start(bf16[3,128]{1,0:T(4,128)(2,1)S(1)} %bitcast.397), channel_id=1, source_target_pairs={{12,0},{14,2},{16,4},{18,6},{20,8},{22,10},{24,12},{26,14},{28,16}... | collective-permute-start | bytes 2312 | tf_op jit(solution)/shard_map/ppermute | solution.py:18
  12.2 81.1 %collective-permute-start.28 = (bf16[3,128]{1,0:T(4,128)(2,1)S(1)}, bf16[3,128]{1,0:T(4,128)(2,1)S(1)}, u32[]{:S(2)}, u32[]{:S(2)}) collective-permute-start(bf16[3,128]{1,0:T(4,128)(2,1)S(1)} %bitcast.398), channel_id=1, source_target_pairs={{10,0},{12,2},{14,4},{16,6},{18,8},{20,10},{22,12},{24,14},{26,16}... | collective-permute-start | bytes 2312 | tf_op jit(solution)/shard_map/ppermute | solution.py:18
  13.5 79.3 %collective-permute-start.27 = (bf16[3,128]{1,0:T(4,128)(2,1)S(1)}, bf16[3,128]{1,0:T(4,128)(2,1)S(1)}, u32[]{:S(2)}, u32[]{:S(2)}) collective-permute-start(bf16[3,128]{1,0:T(4,128)(2,1)S(1)} %bitcast.399), channel_id=1, source_target_pairs={{8,0},{10,2},{12,4},{14,6},{16,8},{18,10},{20,12},{22,14},{24,16},... | collective-permute-start | bytes 2312 | tf_op jit(solution)/shard_map/ppermute | solution.py:18
  24.5 1230.1 %reduce-scatter.17.cloned.1.call-start = ((), (), s32[]{:S(2)}) async-start(), calls=%async_computation.14 | async-start | bytes 2506752 | tf_op jit(solution)/shard_map/reduce_scatter | solution.py:351
  97.7 34.0 %collective-permute-start.32 = (bf16[128,768]{1,0:T(8,128)(2,1)S(1)}, bf16[128,768]{1,0:T(8,128)(2,1)S(1)}, u32[]{:S(2)}, u32[]{:S(2)}) collective-permute-start(bf16[128,768]{1,0:T(8,128)(2,1)S(1)} %get-tuple-element.788), channel_id=1, source_target_pairs={{0,16},{2,18},{4,20},{6,22},{8,24},{10,26},{12,28},{14,30},{1,17},... | collective-permute-start | bytes 589832 | tf_op jit(solution)/shard_map/ppermute | solution.py:18
  105.3 145.2 %collective-permute-start.47 = (bf16[128,768]{1,0:T(8,128)(2,1)S(1)}, bf16[128,768]{1,0:T(8,128)(2,1)S(1)}, u32[]{:S(2)}, u32[]{:S(2)}) collective-permute-start(bf16[128,768]{1,0:T(8,128)(2,1)S(1)} %get-tuple-element.788), channel_id=1, source_target_pairs={{16,0},{18,2},{20,4},{22,6},{24,8},{26,10},{28,12},{30,14},{17,1},... | collective-permute-start | bytes 589832 | tf_op jit(solution)/shard_map/ppermute | solution.py:18
  106.6 141.9 %collective-permute-start.46 = (bf16[128,768]{1,0:T(8,128)(2,1)S(1)}, bf16[128,768]{1,0:T(8,128)(2,1)S(1)}, u32[]{:S(2)}, u32[]{:S(2)}) collective-permute-start(bf16[128,768]{1,0:T(8,128)(2,1)S(1)} %get-tuple-element.788), channel_id=1, source_target_pairs={{14,0},{16,2},{18,4},{20,6},{22,8},{24,10},{26,12},{28,14},{30,16}... | collective-permute-start | bytes 589832 | tf_op jit(solution)/shard_map/ppermute | solution.py:18
  107.9 138.6 %collective-permute-start.45 = (bf16[128,768]{1,0:T(8,128)(2,1)S(1)}, bf16[128,768]{1,0:T(8,128)(2,1)S(1)}, u32[]{:S(2)}, u32[]{:S(2)}) collective-permute-start(bf16[128,768]{1,0:T(8,128)(2,1)S(1)} %get-tuple-element.788), channel_id=1, source_target_pairs={{12,0},{14,2},{16,4},{18,6},{20,8},{22,10},{24,12},{26,14},{28,16}... | collective-permute-start | bytes 589832 | tf_op jit(solution)/shard_map/ppermute | solution.py:18
  111.9 22.9 %collective-permute-start.1 = (bf16[128,768]{1,0:T(8,128)(2,1)S(1)}, bf16[128,768]{1,0:T(8,128)(2,1)S(1)}, u32[]{:S(2)}, u32[]{:S(2)}) collective-permute-start(bf16[128,768]{1,0:T(8,128)(2,1)S(1)} %get-tuple-element.789), channel_id=1, source_target_pairs={{0,14},{2,16},{4,18},{6,20},{8,22},{10,24},{12,26},{14,28},{16,30}... | collective-permute-start | bytes 589832 | tf_op jit(solution)/shard_map/ppermute | solution.py:18
  229.5 53.3 %collective-permute-start.15 = (bf16[128,768]{1,0:T(8,128)(2,1)S(1)}, bf16[128,768]{1,0:T(8,128)(2,1)S(1)}, u32[]{:S(2)}, u32[]{:S(2)}) collective-permute-start(bf16[128,768]{1,0:T(8,128)(2,1)S(1)} %get-tuple-element.789), channel_id=1, source_target_pairs={{16,0},{18,2},{20,4},{22,6},{24,8},{26,10},{28,12},{30,14},{17,1},... | collective-permute-start | bytes 589832 | tf_op jit(solution)/shard_map/ppermute | solution.py:18
  244.5 37.6 %collective-permute-start.14 = (bf16[128,768]{1,0:T(8,128)(2,1)S(1)}, bf16[128,768]{1,0:T(8,128)(2,1)S(1)}, u32[]{:S(2)}, u32[]{:S(2)}) collective-permute-start(bf16[128,768]{1,0:T(8,128)(2,1)S(1)} %get-tuple-element.789), channel_id=1, source_target_pairs={{14,0},{16,2},{18,4},{20,6},{22,8},{24,10},{26,12},{28,14},{30,16}... | collective-permute-start | bytes 589832 | tf_op jit(solution)/shard_map/ppermute | solution.py:18
  246.5 35.0 %collective-permute-start.13 = (bf16[128,768]{1,0:T(8,128)(2,1)S(1)}, bf16[128,768]{1,0:T(8,128)(2,1)S(1)}, u32[]{:S(2)}, u32[]{:S(2)}) collective-permute-start(bf16[128,768]{1,0:T(8,128)(2,1)S(1)} %get-tuple-element.789), channel_id=1, source_target_pairs={{12,0},{14,2},{16,4},{18,6},{20,8},{22,10},{24,12},{26,14},{28,16}... | collective-permute-start | bytes 589832 | tf_op jit(solution)/shard_map/ppermute | solution.py:18
  567.2 830.8 %reduce-scatter.15.cloned.1.call-start = ((), (), s32[]{:S(2)}) async-start(), calls=%async_computation.13 | async-start | bytes 7520256 | tf_op jit(solution)/shard_map/reduce_scatter | solution.py:350
  1116.4 21.5 %collective-permute-start.79 = (bf16[128,768]{0,1:T(8,128)(2,1)S(1)}, bf16[128,768]{0,1:T(8,128)(2,1)S(1)}, u32[]{:S(2)}, u32[]{:S(2)}) collective-permute-start(bf16[128,768]{0,1:T(8,128)(2,1)S(1)} %get-tuple-element.770), channel_id=1, source_target_pairs={{0,16},{2,18},{4,20},{6,22},{8,24},{10,26},{12,28},{14,30},{1,17},... | collective-permute-start | bytes 589832 | tf_op jit(solution)/shard_map/ppermute | solution.py:18
  1161.8 26.1 %collective-permute-start.67 = (bf16[128,768]{0,1:T(8,128)(2,1)S(1)}, bf16[128,768]{0,1:T(8,128)(2,1)S(1)}, u32[]{:S(2)}, u32[]{:S(2)}) collective-permute-start(bf16[128,768]{0,1:T(8,128)(2,1)S(1)} %get-tuple-element.782), channel_id=1, source_target_pairs={{0,4},{2,6},{4,8},{6,10},{8,12},{10,14},{12,16},{14,18},{16,20},{1... | collective-permute-start | bytes 589832 | tf_op jit(solution)/shard_map/ppermute | solution.py:18
  1165.3 24.0 %collective-permute-start.66 = (bf16[128,768]{0,1:T(8,128)(2,1)S(1)}, bf16[128,768]{0,1:T(8,128)(2,1)S(1)}, u32[]{:S(2)}, u32[]{:S(2)}) collective-permute-start(bf16[128,768]{0,1:T(8,128)(2,1)S(1)} %get-tuple-element.783), channel_id=1, source_target_pairs={{4,0},{6,2},{8,4},{10,6},{12,8},{14,10},{16,12},{18,14},{20,16},{2... | collective-permute-start | bytes 589832 | tf_op jit(solution)/shard_map/ppermute | solution.py:18
  1168.6 22.0 %collective-permute-start.65 = (bf16[128,768]{0,1:T(8,128)(2,1)S(1)}, bf16[128,768]{0,1:T(8,128)(2,1)S(1)}, u32[]{:S(2)}, u32[]{:S(2)}) collective-permute-start(bf16[128,768]{0,1:T(8,128)(2,1)S(1)} %get-tuple-element.784), channel_id=1, source_target_pairs={{0,2},{2,4},{4,6},{6,8},{8,10},{10,12},{12,14},{14,16},{16,18},{18... | collective-permute-start | bytes 589832 | tf_op jit(solution)/shard_map/ppermute | solution.py:18
  1172.6 19.3 collective-permute-start.48
  1173.9 22.6 %collective-permute-start.63 = (bf16[128,768]{0,1:T(8,128)(2,1)S(1)}, bf16[128,768]{0,1:T(8,128)(2,1)S(1)}, u32[]{:S(2)}, u32[]{:S(2)}) collective-permute-start(bf16[128,768]{0,1:T(8,128)(2,1)S(1)} %get-tuple-element.754), channel_id=1, source_target_pairs={{0,16},{2,18},{4,20},{6,22},{8,24},{10,26},{12,28},{14,30},{1,17},... | collective-permute-start | bytes 589832 | tf_op jit(solution)/shard_map/ppermute | solution.py:18
  1191.9 20.6 %collective-permute-start.59 = (bf16[128,768]{0,1:T(8,128)(2,1)S(1)}, bf16[128,768]{0,1:T(8,128)(2,1)S(1)}, u32[]{:S(2)}, u32[]{:S(2)}) collective-permute-start(bf16[128,768]{0,1:T(8,128)(2,1)S(1)} %get-tuple-element.758), channel_id=1, source_target_pairs={{0,12},{2,14},{4,16},{6,18},{8,20},{10,22},{12,24},{14,26},{16,28}... | collective-permute-start | bytes 589832 | tf_op jit(solution)/shard_map/ppermute | solution.py:18
  1241.7 332.8 %reduce-scatter.19.cloned.1.call-start = ((), (), s32[]{:S(2)}) async-start(), calls=%async_computation.15 | async-start | bytes 10027008 | tf_op jit(solution)/shard_map/reduce_scatter | solution.py:352
  1247.9 502.2 %reduce-scatter.21.cloned.1.call-start = ((), (), s32[]{:S(2)}) async-start(), calls=%async_computation.16 | async-start | bytes 10027008 | tf_op jit(solution)/shard_map/reduce_scatter | solution.py:353
  1254.6 539.8 %reduce-scatter.27.cloned.1.call-start = ((), (), s32[]{:S(2)}) async-start(), calls=%async_computation.19 | async-start | bytes 294912
  1256.4 539.6 %reduce-scatter.25.cloned.1.call-start = ((), (), s32[]{:S(2)}) async-start(), calls=%async_computation.18 | async-start | bytes 589824
  1400.0 397.7 %reduce-scatter.29.cloned.1.call-start = ((), (), s32[]{:S(2)}) async-start(), calls=%async_computation.20 | async-start | bytes 589824
  1576.5 223.1 %reduce-scatter.23.cloned.1.call-start = ((), (), s32[]{:S(2)}) async-start(), calls=%async_computation.17 | async-start | bytes 442368 | tf_op jit(solution)/shard_map/reduce_scatter | solution.py:365
  1752.0 176.9 %all-reduce.3.cloned.1.call-start = ((), (), s32[]{:S(2)}) async-start(), calls=%async_computation.12 | async-start | bytes 786432 | tf_op jit(solution)/shard_map/psum | solution.py:369
  (272 other events, 5401.2 us)
Sparse Core Ops, SparseCore 0:
  9.6 15.3 all-gather.4
  26.6 10.3 all-gather.6
  38.6 15.5 all-gather.8
  55.6 15.6 all-gather.10
  567.3 133.3 reduce-scatter.16
  1241.8 156.1 reduce-scatter.14
  1404.6 169.7 reduce-scatter.18
  1580.1 170.0 reduce-scatter.20
  1753.1 6.4 reduce-scatter.26
  1761.7 8.9 reduce-scatter.24
  1773.0 8.9 reduce-scatter.28
  1784.7 8.8 reduce-scatter.22
  1800.3 128.5 all-reduce.2
where the time goes:
time: 1950 us; the launch traced here: 1940 us
  waiting for transfers between devices  700 us (36%)
  matrix products  547 us (28%)
  starting transfers between devices  263 us (13%)
  local copies, waits for them, and re-layouts  228 us (12%)
  other arithmetic  136 us (7%)
  blocking collectives  40.6 us (2%)
    ppermute x80, starting transfers between devices, shifted(): return lax.ppermute(x, axis, pairs)  263 us
    dot_general x34, matrix products, shard_logits(): jnp.einsum('qkc,ch->hqk', kernel_low, w_pair, preferred_element_type=jnp....  208 us
    reduce_scatter x1, waiting for transfers between devices, on_device(): lax.psum_scatter(large_grads[2], 'row', scatter_dimension=1, tiled=True)  171 us
    reduce_scatter x1, waiting for transfers between devices, on_device(): lax.psum_scatter(large_grads[3], 'row', scatter_dimension=1, tiled=True)  169 us
    reduce_scatter x1, waiting for transfers between devices, on_device(): lax.psum_scatter(large_grads[0], 'row', scatter_dimension=1, tiled=True)  142 us
    psum x1, waiting for transfers between devices, on_device(): lax.psum((grad_table, gain_part, shift_part, center_part, width_part, pai...  128 us
    dot_general x17, matrix products, backward_step(): jnp.einsum('hqk,ch->qkc', grad_logits, w_pair, preferred_element_type=jnp...  109 us
    ppermute x80, waiting for transfers between devices, shifted(): return lax.ppermute(x, axis, pairs)  88.6 us
  transfers between devices with their start and end apart: 93, of which 31 were waited for; matrix products, arithmetic and copies ran while one was open for 46% of the time, Pallas kernels for 0%

commit v1 on v0

v1 whole, which is shorter than its diff:
```python
import functools
import math

import jax
import jax.numpy as jnp
from jax import lax
from jax.experimental import pallas as pl
from jax.experimental.pallas import tpu as pltpu
from jax.sharding import PartitionSpec as P

MAXLEN = 1024
NEG_FILL = -1e30
HIGHEST = lax.Precision.HIGHEST
QB = 32
TILE = 128
HG = 8
GW = 256
LOG2E = 1.4426950408889634
bf16 = jnp.bfloat16
f32 = jnp.float32


def shifted(x, axis, by):
    length = lax.axis_size(axis)
    pairs = [(i, i + by) for i in range(length) if 0 <= i + by < length]
    return lax.ppermute(x, axis, pairs)


def swap_cores(x):
    return lax.ppermute(x, "wt", [(0, 1), (1, 0)])


def norm_parts(values_in):
    average = jnp.mean(values_in, axis=-1, keepdims=True)
    centred = values_in - average
    inverse = lax.rsqrt(jnp.mean(centred * centred, axis=-1, keepdims=True) + 1e-05)
    return (centred * inverse, inverse)


def norm_back(grad_out, normed, inverse, gain_vec):
    grad_normed = grad_out * gain_vec
    mean_grad = jnp.mean(grad_normed, axis=-1, keepdims=True)
    mean_mixed = jnp.mean(grad_normed * normed, axis=-1, keepdims=True)
    grad_in = inverse * (grad_normed - mean_grad - normed * mean_mixed)
    return (grad_in, jnp.sum(grad_out * normed, axis=0), jnp.sum(grad_out, axis=0))


def gelu_tanh(values_in):
    return (
        0.5
        * values_in
        * (
            1.0
            + jnp.tanh(
                0.7978845608028654 * (values_in + 0.044715 * values_in * values_in * values_in)
            )
        )
    )


def time_code(moment, model_width):
    half_width = model_width // 2
    frequency = jnp.exp(-math.log(10000.0) * jnp.arange(half_width, dtype=jnp.float32) / half_width)
    angles = 100.0 * moment * frequency
    return jnp.concatenate([jnp.sin(angles), jnp.cos(angles)])


def item_ids(places, item_ends):
    return jnp.sum((places[:, None] >= item_ends[None, :]).astype(jnp.int32), axis=1)


def cross_rows(left_side, right_side):
    return lax.dot_general(
        left_side, right_side, (((0,), (0,)), ((), ())), preferred_element_type=jnp.float32
    )


def along_rows(left_side, right_side):
    return lax.dot_general(
        left_side, right_side, (((1,), (1,)), ((), ())), preferred_element_type=jnp.float32
    )


def head_mask(groups_dim):
    h = lax.broadcasted_iota(jnp.int32, (HG, GW), 0)
    f = lax.broadcasted_iota(jnp.int32, (HG, GW), 1)
    lo = h * groups_dim
    return (f >= lo) & (f < lo + groups_dim)


def expand(rows, mask):
    parts = [
        jnp.where(mask, jnp.broadcast_to(rows[i : i + 1, :], (HG, GW)), 0.0)
        for i in range(rows.shape[0])
    ]
    return jnp.concatenate(parts, axis=0)


def collapse(stacked, mask):
    count = stacked.shape[0] // HG
    parts = [
        jnp.sum(jnp.where(mask, stacked[i * HG : (i + 1) * HG, :], 0.0), axis=0, keepdims=True)
        for i in range(count)
    ]
    return jnp.concatenate(parts, axis=0)


def tile_distance(qpos_ref, kpos_ref, tile):
    total = None
    for axis in range(3):
        differ = qpos_ref[:, axis : axis + 1] - kpos_ref[tile, axis : axis + 1, :]
        total = differ * differ if total is None else total + differ * differ
    return jnp.sqrt(total)


def fwd_kernel(
    head_dim, lo_ref, hi_ref, q_ref, kt_ref, v_ref, qpos_ref, kpos_ref, qid_ref, kid_ref,
    cen_ref, amp_ref, lnorm_ref, wpt_ref, p_ref, o_ref, rl_ref,
    qexp, score, top, dist, neg, kern, bias, acc, total,
):
    block = pl.program_id(0)
    lo, hi = lo_ref[block], hi_ref[block]
    groups = wpt_ref.shape[0] // HG
    rows = QB * HG
    scale = head_dim ** (-0.5)
    mask = head_mask(head_dim)
    for g in range(groups):
        qexp[g] = expand(q_ref[:, g * GW : (g + 1) * GW].astype(f32), mask).astype(bf16)
        acc[g] = jnp.zeros((rows, GW), f32)
    top[...] = jnp.full(top.shape, NEG_FILL, f32)
    total[...] = jnp.zeros(total.shape, f32)

    def first(tile, carry):
        dist[...] = tile_distance(qpos_ref, kpos_ref, tile)
        neg[...] = jnp.where(qid_ref[:, 0:1] == kid_ref[tile], 0.0, NEG_FILL)

        def some_kernels(cg, carry):
            at = pl.ds(pl.multiple_of(cg * 16, 16), 16)
            cen, amp, lnorm = cen_ref[at, :], amp_ref[at, :], lnorm_ref[at, :]
            for i in range(QB):
                t = (dist[i : i + 1, :] - cen) * amp
                kern[at, i * TILE : (i + 1) * TILE] = jnp.exp2(lnorm - t * t).astype(bf16)
            return carry

        lax.fori_loop(0, cen_ref.shape[0] // 16, some_kernels, 0)
        for part in range(QB // 8):
            at = slice(part * 8 * TILE, (part + 1) * 8 * TILE)
            bias[:, at] = jnp.dot(wpt_ref[...], kern[:, at], preferred_element_type=f32)
        for g in range(groups):
            dots = jnp.dot(qexp[g], kt_ref[tile, g * GW : (g + 1) * GW, :], preferred_element_type=f32)
            for i in range(QB):
                here = slice(g * rows + i * HG, g * rows + (i + 1) * HG)
                value = (
                    dots[i * HG : (i + 1) * HG, :] * scale
                    + bias[g * HG : (g + 1) * HG, i * TILE : (i + 1) * TILE]
                    + neg[i : i + 1, :]
                )
                score[tile, here, :] = value
                top[here, :] = jnp.maximum(top[here, :], value)
        return carry

    lax.fori_loop(lo, hi, first, 0)
    top[...] = jnp.broadcast_to(jnp.max(top[...], axis=1, keepdims=True), top.shape)

    def second(tile, carry):
        for g in range(groups):
            here = slice(g * rows, (g + 1) * rows)
            prob = jnp.exp(score[tile, here, :] - top[here, :])
            total[here, :] += prob
            low = prob.astype(bf16)
            p_ref[0, tile, here, :] = low
            acc[g] += jnp.dot(low, v_ref[tile, :, g * GW : (g + 1) * GW], preferred_element_type=f32)
        return carry

    lax.fori_loop(lo, hi, second, 0)
    for g in range(groups):
        here = slice(g * rows, (g + 1) * rows)
        inverse = 1.0 / jnp.sum(total[here, :], axis=1, keepdims=True)
        rl_ref[here, :] = jnp.broadcast_to(inverse, (rows, TILE))
        o_ref[:, g * GW : (g + 1) * GW] = collapse(acc[g] * inverse, mask)


def bwd_kernel(
    head_dim, lo_ref, hi_ref, p_ref, rl_ref, q_ref, do_ref, o_ref, k_ref, vt_ref, qpos_ref, kpos_ref,
    cen_ref, amp_ref, lnorm_ref, wp_ref, dq_ref, dkt_ref, dvt_ref, m0_ref, sums_ref,
    qext, doexp, doext, delta, dqacc, glow, dist, kern, gk,
):
    block = pl.program_id(0)
    lo, hi = lo_ref[block], hi_ref[block]
    groups = q_ref.shape[1] // GW
    rows = QB * HG
    mask = head_mask(head_dim)

    @pl.when(block == 0)
    def _():
        dkt_ref[...] = jnp.zeros(dkt_ref.shape, f32)
        dvt_ref[...] = jnp.zeros(dvt_ref.shape, f32)
        m0_ref[...] = jnp.zeros(m0_ref.shape, f32)
        sums_ref[...] = jnp.zeros(sums_ref.shape, f32)

    for g in range(groups):
        lanes = slice(g * GW, (g + 1) * GW)
        here = slice(g * rows, (g + 1) * rows)
        inverse = rl_ref[here, 0:1]
        qext[g] = jnp.transpose(expand(q_ref[:, lanes].astype(f32), mask)).astype(bf16)
        grads = do_ref[:, lanes].astype(f32)
        both = expand(grads, mask) * inverse
        doexp[g] = both.astype(bf16)
        doext[g] = jnp.transpose(both).astype(bf16)
        mixed = jnp.sum(expand(grads * o_ref[:, lanes], mask), axis=1, keepdims=True) * inverse
        delta[here, :] = jnp.broadcast_to(mixed, (rows, TILE))
        dqacc[g] = jnp.zeros((rows, GW), f32)

    def one_tile(tile, carry):
        dist[...] = tile_distance(qpos_ref, kpos_ref, tile)
        for pair in range(groups // 2):
            grads = []
            for g in (2 * pair, 2 * pair + 1):
                lanes = slice(g * GW, (g + 1) * GW)
                here = slice(g * rows, (g + 1) * rows)
                low = p_ref[0, tile, here, :]
                dp = jnp.dot(doexp[g], vt_ref[tile, lanes, :], preferred_element_type=f32)
                gl = low.astype(f32) * (dp - delta[here, :])
                grads.append(gl)
                gl_low = gl.astype(bf16)
                dqacc[g] += jnp.dot(gl_low, k_ref[tile, :, lanes], preferred_element_type=f32)
                dkt_ref[tile, lanes, :] += jnp.dot(qext[g], gl_low, preferred_element_type=f32)
                dvt_ref[tile, lanes, :] += jnp.dot(doext[g], low, preferred_element_type=f32)
            for i in range(QB):
                at = slice(i * HG, (i + 1) * HG)
                glow[pair * 16 : (pair + 1) * 16, i * TILE : (i + 1) * TILE] = jnp.concatenate(
                    [grads[0][at, :], grads[1][at, :]], axis=0
                ).astype(bf16)
        for part in range(QB // 8):
            at = slice(part * 8 * TILE, (part + 1) * 8 * TILE)
            gk[:, at] = jnp.dot(wp_ref[...], glow[:, at], preferred_element_type=f32)

        def some_kernels(cg, carry):
            at = pl.ds(pl.multiple_of(cg * 16, 16), 16)
            cen, amp, lnorm = cen_ref[at, :], amp_ref[at, :], lnorm_ref[at, :]
            plain = jnp.zeros((16, TILE), f32)
            once = jnp.zeros((16, TILE), f32)
            twice = jnp.zeros((16, TILE), f32)
            for i in range(QB):
                lanes = slice(i * TILE, (i + 1) * TILE)
                t = (dist[i : i + 1, :] - cen) * amp
                value = jnp.exp2(lnorm - t * t)
                kern[at, lanes] = value.astype(bf16)
                weighted = gk[at, lanes] * value
                plain = plain + weighted
                weighted = weighted * t
                once = once + weighted
                twice = twice + weighted * t
            sums_ref[0, at, :] += plain
            sums_ref[1, at, :] += once
            sums_ref[2, at, :] += twice
            return carry

        lax.fori_loop(0, cen_ref.shape[0] // 16, some_kernels, 0)
        m0_ref[...] += lax.dot_general(
            glow[...], kern[...], (((1,), (1,)), ((), ())), preferred_element_type=f32
        )
        return carry

    lax.fori_loop(lo, hi, one_tile, 0)
    for g in range(groups):
        dq_ref[:, g * GW : (g + 1) * GW] = collapse(dqacc[g], mask)


def whole(shape):
    return pl.BlockSpec(shape, lambda *_: (0,) * len(shape), pipeline_mode=pl.Buffered(1))


def attention_forward(lo, hi, q, kt, v, qpos, kpos, qid, kid, cen, amp, lnorm, wpt, head_dim):
    tiles = kt.shape[0]
    wide = q.shape[1]
    groups = wide // GW
    rows = QB * HG
    blocks = q.shape[0] // QB
    kernels, heads = cen.shape[0], wpt.shape[0]
    by_block = lambda b, *_: (b, 0)
    return pl.pallas_call(
        functools.partial(fwd_kernel, head_dim),
        grid_spec=pltpu.PrefetchScalarGridSpec(
            num_scalar_prefetch=2,
            grid=(blocks,),
            in_specs=[
                pl.BlockSpec((QB, wide), by_block),
                whole(kt.shape),
                whole(v.shape),
                pl.BlockSpec((QB, 3), by_block),
                whole(kpos.shape),
                pl.BlockSpec((QB, 1), by_block),
                whole(kid.shape),
                whole(cen.shape),
                whole(amp.shape),
                whole(lnorm.shape),
                whole(wpt.shape),
            ],
            out_specs=[
                pl.BlockSpec((1, tiles, groups * rows, TILE), lambda b, *_: (b, 0, 0, 0)),
                pl.BlockSpec((QB, wide), by_block),
                pl.BlockSpec((groups * rows, TILE), by_block),
            ],
            scratch_shapes=[
                pltpu.VMEM((groups, rows, GW), bf16),
                pltpu.VMEM((tiles, groups * rows, TILE), f32),
                pltpu.VMEM((groups * rows, TILE), f32),
                pltpu.VMEM((QB, TILE), f32),
                pltpu.VMEM((QB, TILE), f32),
                pltpu.VMEM((kernels, QB * TILE), bf16),
                pltpu.VMEM((heads, QB * TILE), f32),
                pltpu.VMEM((groups, rows, GW), f32),
                pltpu.VMEM((groups * rows, TILE), f32),
            ],
        ),
        out_shape=[
            jax.ShapeDtypeStruct((blocks, tiles, groups * rows, TILE), bf16),
            jax.ShapeDtypeStruct(q.shape, f32),
            jax.ShapeDtypeStruct((blocks * groups * rows, TILE), f32),
        ],
        compiler_params=pltpu.CompilerParams(vmem_limit_bytes=60 << 20),
        name="attend",
    )(lo, hi, q, kt, v, qpos, kpos, qid, kid, cen, amp, lnorm, wpt)


def attention_backward(lo, hi, p, rl, q, do, o, k, vt, qpos, kpos, cen, amp, lnorm, wp, head_dim):
    tiles = vt.shape[0]
    wide = q.shape[1]
    groups = wide // GW
    rows = QB * HG
    blocks = q.shape[0] // QB
    kernels, heads = wp.shape
    by_block = lambda b, *_: (b, 0)
    return pl.pallas_call(
        functools.partial(bwd_kernel, head_dim),
        grid_spec=pltpu.PrefetchScalarGridSpec(
            num_scalar_prefetch=2,
            grid=(blocks,),
            in_specs=[
                pl.BlockSpec((1, tiles, groups * rows, TILE), lambda b, *_: (b, 0, 0, 0)),
                pl.BlockSpec((groups * rows, TILE), by_block),
                pl.BlockSpec((QB, wide), by_block),
                pl.BlockSpec((QB, wide), by_block),
                pl.BlockSpec((QB, wide), by_block),
                whole(k.shape),
                whole(vt.shape),
                pl.BlockSpec((QB, 3), by_block),
                whole(kpos.shape),
                whole(cen.shape),
                whole(amp.shape),
                whole(lnorm.shape),
                whole(wp.shape),
            ],
            out_specs=[
                pl.BlockSpec((QB, wide), by_block),
                whole(vt.shape),
                whole(vt.shape),
                whole((heads, kernels)),
                whole((3, kernels, TILE)),
            ],
            scratch_shapes=[
                pltpu.VMEM((groups, GW, rows), bf16),
                pltpu.VMEM((groups, rows, GW), bf16),
                pltpu.VMEM((groups, GW, rows), bf16),
                pltpu.VMEM((groups * rows, TILE), f32),
                pltpu.VMEM((groups, rows, GW), f32),
                pltpu.VMEM((heads, QB * TILE), bf16),
                pltpu.VMEM((QB, TILE), f32),
                pltpu.VMEM((kernels, QB * TILE), bf16),
                pltpu.VMEM((kernels, QB * TILE), f32),
            ],
        ),
        out_shape=[
            jax.ShapeDtypeStruct(q.shape, f32),
            jax.ShapeDtypeStruct(vt.shape, f32),
            jax.ShapeDtypeStruct(vt.shape, f32),
            jax.ShapeDtypeStruct((heads, kernels), f32),
            jax.ShapeDtypeStruct((3, kernels, TILE), f32),
        ],
        compiler_params=pltpu.CompilerParams(vmem_limit_bytes=60 << 20),
        name="attend_back",
    )(lo, hi, p, rl, q, do, o, k, vt, qpos, kpos, cen, amp, lnorm, wp)


def on_device(
    atoms,
    coords,
    atom_types,
    lengths,
    times,
    type_table,
    gain_one,
    shift_one,
    w_qkv,
    centers,
    widths,
    w_pair,
    w_out,
    gain_two,
    shift_two,
    w_up,
    w_down,
    w_force,
    out_grad,
    force_grad,
):
    micro_count, row_count, model_width = atoms.shape
    head_count = w_pair.shape[1]
    head_dim = model_width // head_count
    score_scale = head_dim ** (-0.5)
    my_index = lax.axis_index("row")
    my_core = lax.axis_index("wt")
    row_size = lax.axis_size("row")
    reach_shards = (MAXLEN - 2) // row_count + 1
    all_rows = row_count * row_size
    groups = head_count // HG
    used = HG * head_dim
    covers = row_size <= 2 * reach_shards + 1
    span = row_size if covers else 2 * reach_shards + 1
    key_count = span * row_count
    key_base = 0 if covers else (my_index - reach_shards) * row_count
    type_codes = jnp.arange(type_table.shape[0], dtype=jnp.int32)

    def fetch(x, axis):
        if covers:
            return lax.all_gather(x, "row", axis=axis, tiled=True)
        far = [shifted(x, "row", by) for by in range(reach_shards, 0, -1)]
        near = [shifted(x, "row", -by) for by in range(1, reach_shards + 1)]
        return jnp.concatenate(far + [x] + near, axis=axis)

    def send_back(x):
        if covers:
            return lax.psum_scatter(x.astype(bf16), "row", scatter_dimension=0, tiled=True).astype(f32)
        shards = x.reshape(span, row_count, model_width)
        own = shards[reach_shards]
        for offset in range(1, reach_shards + 1):
            for by in (offset, -offset):
                own = own + shifted(shards[reach_shards - by].astype(bf16), "row", -by).astype(f32)
        return own

    def padded(x, axis):
        split = x.reshape(x.shape[:axis] + (groups, used) + x.shape[axis + 1 :])
        pads = [(0, 0)] * split.ndim
        pads[axis + 1] = (0, GW - used)
        return jnp.pad(split, pads).reshape(x.shape[:axis] + (groups * GW,) + x.shape[axis + 1 :])

    def unpadded(x, axis):
        split = x.reshape(x.shape[:axis] + (groups, GW) + x.shape[axis + 1 :])
        split = lax.slice_in_dim(split, 0, used, axis=axis + 1)
        return split.reshape(x.shape[:axis] + (groups * used,) + x.shape[axis + 1 :])

    w_qkv_full = lax.all_gather(w_qkv, "wt", axis=0, tiled=True)
    w_out_full = lax.all_gather(w_out, "wt", axis=0, tiled=True)
    w_up_full = lax.all_gather(w_up, "wt", axis=0, tiled=True)
    w_down_full = lax.all_gather(w_down, "wt", axis=0, tiled=True)
    w_q = padded(w_qkv_full[:, :model_width], 1)
    w_k = padded(w_qkv_full[:, model_width : 2 * model_width], 1)
    w_v = padded(w_qkv_full[:, 2 * model_width :], 1)

    item_ends = jnp.cumsum(lengths[0])
    own_places = my_index * row_count + jnp.arange(row_count, dtype=jnp.int32)
    own_ids = item_ids(own_places, item_ends)
    key_places = key_base + jnp.arange(key_count, dtype=jnp.int32)
    inside = (key_places >= 0) & (key_places < all_rows)
    key_ids = jnp.where(inside, item_ids(key_places, item_ends), -1)
    first_places = own_places[::QB]
    last_places = own_places[QB - 1 :: QB]
    begins = jnp.max(jnp.where(item_ends[None, :] <= first_places[:, None], item_ends[None, :], 0), axis=1)
    ends = jnp.min(
        jnp.where(item_ends[None, :] > last_places[:, None], item_ends[None, :], all_rows), axis=1
    )
    tiles = key_count // TILE
    lo = jnp.clip((begins - key_base) // TILE, 0, tiles)
    hi = jnp.clip((ends - key_base + TILE - 1) // TILE, 0, tiles)

    onehot = (atom_types[0][:, None] == type_codes[None, :]).astype(bf16)
    base_rows = (
        atoms[0].astype(f32)
        + time_code(times[0], model_width)
        + jnp.dot(onehot, type_table, preferred_element_type=f32)
    )
    normed_one, inverse_one = norm_parts(base_rows)
    normed_in = (normed_one * gain_one + shift_one).astype(bf16)
    every = fetch(normed_in, 0)
    positions = fetch(coords[:, 0, :], 1).astype(f32)

    queries = jnp.dot(normed_in, w_q, preferred_element_type=f32).astype(bf16)
    keys = jnp.dot(every, w_k, preferred_element_type=f32).astype(bf16)
    values = jnp.dot(every, w_v, preferred_element_type=f32).astype(bf16)
    wide = groups * GW
    by_tile = lambda x: x.reshape(tiles, TILE, wide)
    keys, values = by_tile(keys), by_tile(values)
    keys_t = jnp.swapaxes(keys, 1, 2)
    values_t = jnp.swapaxes(values, 1, 2)
    qpos = jnp.transpose(coords[:, 0, :].astype(f32))
    kpos = jnp.swapaxes(positions.reshape(3, tiles, TILE), 0, 1)
    qid = own_ids[:, None]
    kid = key_ids.reshape(tiles, 1, TILE)
    steep = math.sqrt(0.5 * LOG2E)
    lanes = lambda x: jnp.broadcast_to(x[:, None], (x.shape[0], TILE))
    cen, amp = lanes(centers), lanes(steep / widths)
    lnorm = lanes(-jnp.log2(math.sqrt(2.0 * math.pi) * widths))

    probs, att_wide, inverse_total = attention_forward(
        lo, hi, queries, keys_t, values, qpos, kpos, qid, kid, cen, amp, lnorm,
        jnp.transpose(w_pair), head_dim,
    )
    attended = unpadded(att_wide, 1)
    att_low = attended.astype(bf16)
    after_att = base_rows + jnp.dot(att_low, w_out_full, preferred_element_type=f32)
    normed_two, inverse_two = norm_parts(after_att)
    ffn_in = (normed_two * gain_two + shift_two).astype(bf16)
    hidden = jnp.dot(ffn_in, w_up_full, preferred_element_type=f32)
    activated_full, gelu_pull = jax.vjp(gelu_tanh, hidden)
    activated = activated_full.astype(bf16)
    block_sum = after_att + jnp.dot(activated, w_down_full, preferred_element_type=f32)
    out_low = block_sum.astype(bf16)
    force_rows = along_rows(w_force, out_low)
    force_cot = force_grad[:, 0, :]
    grad_sum = out_grad[0].astype(f32) + lax.dot_general(
        force_cot,
        w_force.astype(f32),
        (((0,), (0,)), ((), ())),
        precision=HIGHEST,
        preferred_element_type=f32,
    )
    grad_force = jnp.dot(
        force_cot, out_low.astype(f32), precision=HIGHEST, preferred_element_type=f32
    )
    grad_sum_low = grad_sum.astype(bf16)
    grad_act_low = along_rows(grad_sum_low, w_down_full).astype(bf16)
    grad_hidden_low = gelu_pull(grad_act_low.astype(f32))[0].astype(bf16)
    grad_ffn_in = along_rows(grad_hidden_low, w_up_full)
    grad_norm_two, grad_gain_two, grad_shift_two = norm_back(
        grad_ffn_in, normed_two, inverse_two, gain_two
    )
    grad_after = grad_sum + grad_norm_two
    grad_after_low = grad_after.astype(bf16)
    grad_att_low = along_rows(grad_after_low, w_out_full).astype(bf16)

    def my_half(x):
        half = x.shape[1] // 2
        return jnp.where(my_core == 0, x[:, :half], x[:, half:])

    def other_half(x):
        half = x.shape[1] // 2
        return jnp.where(my_core == 0, x[:, half:], x[:, :half])

    def weight_grad(left, right):
        lefts = jnp.concatenate([my_half(left), swap_cores(other_half(left))], axis=0)
        rights = jnp.concatenate([right, swap_cores(right)], axis=0)
        return cross_rows(lefts, rights).astype(bf16)

    def over_rows(x):
        return lax.psum_scatter(x, "row", scatter_dimension=1, tiled=True).astype(f32)

    w_down_grad = over_rows(weight_grad(activated, grad_sum_low))
    w_up_grad = over_rows(weight_grad(ffn_in, grad_hidden_low))
    w_out_grad = over_rows(weight_grad(att_low, grad_after_low))

    dq, dkt, dvt, pair_t, kernel_sums = attention_backward(
        lo, hi, probs, inverse_total, queries, padded(grad_att_low, 1), att_wide, keys, values_t,
        qpos, kpos, cen, amp, lnorm, w_pair, head_dim,
    )
    query_grad = (dq * score_scale).astype(bf16)
    key_grad = (jnp.swapaxes(dkt, 1, 2).reshape(key_count, wide) * score_scale).astype(bf16)
    value_grad = jnp.swapaxes(dvt, 1, 2).reshape(key_count, wide).astype(bf16)
    grad_every = along_rows(key_grad, w_k) + along_rows(value_grad, w_v)
    grad_normed_in = along_rows(query_grad, w_q) + send_back(grad_every)
    qkv_grad_w = jnp.concatenate(
        [
            unpadded(cross_rows(normed_in, query_grad), 1),
            unpadded(cross_rows(every, key_grad), 1),
            unpadded(cross_rows(every, value_grad), 1),
        ],
        axis=1,
    ).astype(bf16)
    w_qkv_grad = over_rows(lax.psum_scatter(qkv_grad_w, "wt", scatter_dimension=0, tiled=True))
    grad_norm_one, grad_gain_one, grad_shift_one = norm_back(
        grad_normed_in, normed_one, inverse_one, gain_one
    )
    atoms_grad = grad_after + grad_norm_one
    grad_table = lax.dot_general(
        onehot.astype(f32),
        atoms_grad,
        (((0,), (0,)), ((), ())),
        precision=HIGHEST,
        preferred_element_type=f32,
    )
    sums = jnp.sum(kernel_sums, axis=2)
    center_part = sums[1] / (steep * widths)
    width_part = (sums[2] / (steep * steep) - sums[0]) / widths
    small_sums = lax.psum(
        (
            grad_table,
            grad_gain_one,
            grad_shift_one,
            center_part,
            width_part,
            jnp.transpose(pair_t),
            grad_gain_two,
            grad_shift_two,
            grad_force,
        ),
        ("row", "wt"),
    )
    return (
        out_low[None],
        force_rows[:, None, :],
        atoms_grad[None],
        small_sums[0],
        small_sums[1],
        small_sums[2],
        w_qkv_grad,
        small_sums[3],
        small_sums[4],
        small_sums[5],
        w_out_grad,
        small_sums[6],
        small_sums[7],
        w_up_grad,
        w_down_grad,
        small_sums[8],
    )


def solution(mesh):
    in_specs = (
        P("wt", "row", None),
        P(None, "wt", "row"),
        P("wt", "row"),
        P("wt", None),
        P("wt"),
        P(),
        P(),
        P(),
        P("wt", None),
        P(),
        P(),
        P(),
        P("wt", None),
        P(),
        P(),
        P("wt", None),
        P("wt", None),
        P(),
        P("wt", "row", None),
        P(None, "wt", "row"),
    )
    out_specs = (
        P("wt", "row", None),
        P(None, "wt", "row"),
        P("wt", "row", None),
        P(),
        P(),
        P(),
        P("wt", "row"),
        P(),
        P(),
        P(),
        P("wt", "row"),
        P(),
        P(),
        P("wt", "row"),
        P("wt", "row"),
        P(),
    )
    return jax.shard_map(
        on_device, mesh=mesh, in_specs=in_specs, out_specs=out_specs, check_vma=False
    )
```

time: 1950 us -> 1220 us (0.63)
  matrix products: 547 us -> 73.7 us
  starting transfers between devices: 263 us -> 2.77 us
  waiting for transfers between devices: 700 us -> 877 us
  local copies, waits for them, and re-layouts: 228 us -> 83.6 us
  other arithmetic: 136 us -> 29.8 us
  Pallas kernels: 0 us -> 48.2 us
  blocking collectives: 40.6 us -> 84.2 us
    dot_general x195 -> x10, matrix products: 519 us -> 29.5 us  [the longest x1 7.88 us: on_device(): values = jnp.dot(every, w_v, preferred_element_type=f32).astype(bf16)]
    ppermute x80 -> x6, starting transfers between devices: 263 us -> 1.99 us  [swap_cores(): return lax.ppermute(x, 'wt', [(0, 1), (1, 0)])]
    reduce_scatter x5, waiting for transfers between devices: 482 us -> 603 us  [the longest x4 474 us: over_rows(): lax.psum_scatter(x, 'row', scatter_dimension=1, tiled=True).astype(f32)]
    unnamed x16 -> x13, waiting for transfers between devices: 2.23 us -> 111 us
    ppermute x80 -> x6, waiting for transfers between devices: 88.6 us -> 3.7 us  [swap_cores(): return lax.ppermute(x, 'wt', [(0, 1), (1, 0)])]
    dynamic_slice x85 -> x0, local copies, waits for them, and re-layouts: 73.8 us -> none  [on_device(): lax.scan(forward_step, start_state, shards_in)]
    dot_general x34 -> x2, local copies, waits for them, and re-layouts: 68.3 us -> 13.2 us  [cross_rows(): lax.dot_general(left_side, right_side, (((0,), (0,)), ((), ())), preferre...]
    pallas_call x0 -> x2, Pallas kernels: none -> 48.2 us  [the longest x1 31.9 us: attention_backward(): pl.pallas_call(functools.partial(bwd_kernel, head_dim), grid_spec=pltpu.P...]
  transfers between devices with their start and end apart: 93 -> 18, of which waited for: 31 -> 12; matrix products, arithmetic and copies ran while one was open for 46% -> 8% of each run, Pallas kernels for 0% -> 1%
where the time goes in v1:
time: 1220 us
  waiting for transfers between devices  877 us (72%)
  blocking collectives  84.2 us (7%)
  local copies, waits for them, and re-layouts  83.6 us (7%)
  matrix products  73.7 us (6%)
  Pallas kernels  48.2 us (4%)
  other arithmetic  29.8 us (2%)
  between operations  16.1 us (1%)
    reduce_scatter x4, waiting for transfers between devices, over_rows(): lax.psum_scatter(x, 'row', scatter_dimension=1, tiled=True).astype(f32)  474 us
    psum x1, waiting for transfers between devices, on_device(): lax.psum((grad_table, grad_gain_one, grad_shift_one, center_part, width_p...  130 us
    reduce_scatter x1, waiting for transfers between devices, send_back(): lax.psum_scatter(x.astype(bf16), 'row', scatter_dimension=0, tiled=True)  129 us
    unnamed x13, waiting for transfers between devices  111 us
    all_gather x1, blocking collectives, fetch(): return lax.all_gather(x, 'row', axis=axis, tiled=True)  42.4 us
    psum x1, blocking collectives, on_device(): lax.psum((grad_table, grad_gain_one, grad_shift_one, center_part, width_p...  41.8 us
    pallas_call x1, Pallas kernels, attention_backward(): pl.pallas_call(functools.partial(bwd_kernel, head_dim), grid_spec=pltpu.P...  31.9 us
    all_gather x1, waiting for transfers between devices, fetch(): return lax.all_gather(x, 'row', axis=axis, tiled=True)  29.1 us
  transfers between devices with their start and end apart: 18, of which 12 were waited for; matrix products, arithmetic and copies ran while one was open for 8% of the time, Pallas kernels for 1%

profile of v1, /device:TPU:0, one launch (start us, length us, event | category | flops | bytes accessed | tf_op | source)
XLA Modules:
  0.0 1215.8 jit_solution(14576985301253886660)
XLA Ops:
  7.2 3.9 copy.81
  15.9 42.4 %all-gather = bf16[3,1,2048]{2,0,1:T(4,128)(2,1)S(1)} all-gather(bf16[3,1,128]{2,0,1:T(4,128)(2,1)S(1)} %copy-done.39), channel_id=2, replica_groups=mesh['row'=16,'wt'=2] {'row'}, dimensions={2}, use_global_device_ids=true | all-gather | bytes 13056 | tf_op jit(solution)/shard_map/all_gather | solution.py:427
  70.2 29.1 %all-gather.9.cloned.1.call-done = bf16[2048,768]{1,0:T(8,128)(2,1)} async-done(((bf16[128,768]{1,0:T(8,128)(2,1)}), bf16[2048,768]{1,0:T(8,128)(2,1)}) %all-gather.9.cloned.1.call-update) | async-done | bytes 3145744 | tf_op jit(solution)/shard_map/all_gather | solution.py:427
  99.4 7.8 convolution_convert_fusion.2
  107.2 6.6 copy.83.kt_ref
  113.8 7.9 convolution_convert_fusion.1
  121.7 6.4 copy.88
  130.1 16.3 %attend.1 = (bf16[4,16,1024,128]{3,2,1,0:T(8,128)(2,1)}, f32[128,1024]{1,0:T(8,128)}, f32[4096,128]{1,0:T(8,128)}) custom-call(s32[4]{0:T(128)} %get-tuple-element.144.lo_ref, s32[4]{0:T(128)} %get-tuple-element.143.hi_ref, bf16[128,1024]{1,0:T(8,128)(2,1)} %convolution_convert_fusion.7.q_ref, bf16[16,1024,128]{2,1,0:T(8,128)(2,1)} %copy.83.kt_ref, ...), custom_call_target="tpu_custom_call" | custom-call | tf_op jit(solution)/shard_map/attend/pallas_call | solution.py:282
  150.5 4.8 multiply_convert_fusion.1
  155.3 5.3 fusion.9
  171.0 31.9 %attend_back.1 = (f32[128,1024]{1,0:T(8,128)}, f32[16,1024,128]{2,1,0:T(8,128)}, f32[16,1024,128]{2,1,0:T(8,128)}, f32[32,128]{1,0:T(8,128)}, f32[3,128,128]{2,1,0:T(8,128)}) custom-call(s32[4]{0:T(128)} %get-tuple-element.144.lo_ref, s32[4]{0:T(128)} %get-tuple-element.143.hi_ref, bf16[4,16,1024,128]{3,2,1,0:T(8,128)(2,1)} %get-tuple-element.25.p_ref, ...), custom_call_target="tpu_custom_call" | custom-call | tf_op jit(solution)/shard_map/attend_back/pallas_call | solution.py:335
  203.0 6.5 fusion
  209.4 6.3 copy.90
  215.7 6.1 convert_bitcast_fusion
  221.8 6.3 copy.91
  228.1 6.5 copy.101
  234.6 6.6 fusion.2
  242.3 6.7 copy.100
  249.1 6.6 fusion.4
  258.6 3.9 reshape.229
  269.5 5.8 copy.102
  275.4 5.8 fusion.53
  281.2 4.8 add_convert_fusion
  304.2 109.5 %reduce-scatter.19.cloned.1.call-done = bf16[384,2304]{1,0:T(8,128)(2,1)} async-done(((bf16[768,2304]{1,0:T(8,128)(2,1)}), bf16[384,2304]{1,0:T(8,128)(2,1)}) %reduce-scatter.19.cloned.1.call-update) | async-done | bytes 1769488
  413.7 3.9 copy.103
  422.2 129.1 %reduce-scatter.9.cloned.1.call-done = bf16[128,768]{1,0:T(8,128)(2,1)} async-done(((bf16[2048,768]{1,0:T(8,128)(2,1)}), bf16[128,768]{1,0:T(8,128)(2,1)}) %reduce-scatter.9.cloned.1.call-update) | async-done | bytes 196624 | tf_op jit(solution)/shard_map/reduce_scatter | solution.py:434
  554.5 123.7 %reduce-scatter.13.cloned.1.call-done = bf16[384,48]{0,1:T(8,128)(2,1)} async-done(((bf16[384,768]{0,1:T(8,128)(2,1)}), bf16[384,48]{0,1:T(8,128)(2,1)}) %reduce-scatter.13.cloned.1.call-update) | async-done | bytes 36880 | tf_op jit(solution)/shard_map/reduce_scatter | solution.py:556
  679.7 130.9 %reduce-scatter.17.cloned.1.call-done = bf16[1536,48]{0,1:T(8,128)(2,1)} async-done(((bf16[1536,768]{0,1:T(8,128)(2,1)}), bf16[1536,48]{0,1:T(8,128)(2,1)}) %reduce-scatter.17.cloned.1.call-update) | async-done | bytes 147472 | tf_op jit(solution)/shard_map/reduce_scatter | solution.py:556
  812.3 131.6 %reduce-scatter.15.cloned.1.call-done = bf16[384,192]{0,1:T(8,128)(2,1)} async-done(((bf16[384,3072]{0,1:T(8,128)(2,1)}), bf16[384,192]{0,1:T(8,128)(2,1)}) %reduce-scatter.15.cloned.1.call-update) | async-done | bytes 147472 | tf_op jit(solution)/shard_map/reduce_scatter | solution.py:556
  945.5 41.8 %all-reduce.4 = (f32[768]{0:T(1024)}, f32[768]{0:T(1024)}, f32[128]{0:T(128)}, f32[128]{0:T(128)}, f32[128,32]{0,1:T(8,128)}, /*index=5*/f32[768]{0:T(1024)}, f32[768]{0:T(1024)}, f32[3,768]{1,0:T(4,128)}) all-reduce(f32[768]{0:T(1024)S(1)} %get-tuple-element.98, ...), channel_id=1, replica_groups=mesh['row'=16,'wt'=2] {'row','wt'}, use_global_device_ids=true, to_apply=%region_16.17 | all-reduce | flops 9728 | bytes 77824 | tf_op jit(solution)/shard_map/psum | solution.py:594
  987.3 87.3 %reduce-scatter.11.cloned.1.call-done = bf16[384,144]{0,1:T(8,128)(2,1)} async-done(((bf16[384,2304]{0,1:T(8,128)(2,1)}), bf16[384,144]{0,1:T(8,128)(2,1)}) %reduce-scatter.11.cloned.1.call-update) | async-done | bytes 110608 | tf_op jit(solution)/shard_map/reduce_scatter | solution.py:556
  1076.2 130.4 %all-reduce.7.cloned.1.call-done = f32[128,768]{1,0:T(8,128)} async-done(((f32[128,768]{1,0:T(8,128)}), f32[128,768]{1,0:T(8,128)}) %all-reduce.7.cloned.1.call-update) | async-done | bytes 393232 | tf_op jit(solution)/shard_map/psum | solution.py:594
  (211 shorter events, 77.1 us)
Async XLA Ops:
  7.2 56.8 %all-gather.7.cloned.1.call-start = ((), (), s32[]{:S(2)}) async-start(), calls=%async_computation.6 | async-start | bytes 5308416 | tf_op jit(solution)/shard_map/all_gather | solution.py:453
  11.2 88.2 %all-gather.9.cloned.1.call-start = ((), (), s32[]{:S(2)}) async-start(), calls=%async_computation.7 | async-start | bytes 3342336 | tf_op jit(solution)/shard_map/all_gather | solution.py:427
  13.5 134.2 %all-gather.11.cloned.1.call-start = ((), (), s32[]{:S(2)}) async-start(), calls=%async_computation.8 | async-start | bytes 1769472 | tf_op jit(solution)/shard_map/all_gather | solution.py:454
  14.3 136.3 %all-gather.13.cloned.1.call-start = ((), (), s32[]{:S(2)}) async-start(), calls=%async_computation.9 | async-start | bytes 7077888 | tf_op jit(solution)/shard_map/all_gather | solution.py:455
  14.9 46.1 %copy-start.44 = (f32[128]{0:T(128)S(1)}, f32[128]{0:T(128)}, u32[]{:S(2)}) copy-start(f32[128]{0:T(128)} %param.30) | copy-start | bytes 1540
  14.9 47.9 %copy-start.18 = (bf16[1,128,768]{2,1,0:T(8,128)(2,1)S(1)}, bf16[1,128,768]{2,1,0:T(8,128)(2,1)}, u32[]{:S(2)}) copy-start(bf16[1,128,768]{2,1,0:T(8,128)(2,1)} %param.38) | copy-start | bytes 589828
  14.9 47.9 %copy-start.23 = (bf16[3,768]{1,0:T(4,128)(2,1)S(1)}, bf16[3,768]{1,0:T(4,128)(2,1)}, u32[]{:S(2)}) copy-start(bf16[3,768]{1,0:T(4,128)(2,1)} %param.37) | copy-start | bytes 13828
  14.9 47.9 %copy-start.27 = (f32[3,1,128]{2,1,0:T(1,128)S(1)}, f32[3,1,128]{2,1,0:T(1,128)}, u32[]{:S(2)}) copy-start(f32[3,1,128]{2,1,0:T(1,128)} %param.39) | copy-start | bytes 4612
  14.9 140.4 %all-gather.15.cloned.1.call-start = ((), (), s32[]{:S(2)}) async-start(), calls=%async_computation.10 | async-start | bytes 7077888 | tf_op jit(solution)/shard_map/all_gather | solution.py:456
  15.5 398.2 %reduce-scatter.19.cloned.1.call-start = ((), (), s32[]{:S(2)}) async-start(), calls=%async_computation.17 | async-start | bytes 5308416
  275.3 276.0 %reduce-scatter.9.cloned.1.call-start = ((), (), s32[]{:S(2)}) async-start(), calls=%async_computation.11 | async-start | bytes 3342336 | tf_op jit(solution)/shard_map/reduce_scatter | solution.py:434
  286.1 392.2 %reduce-scatter.13.cloned.1.call-start = ((), (), s32[]{:S(2)}) async-start(), calls=%async_computation.14 | async-start | bytes 626688 | tf_op jit(solution)/shard_map/reduce_scatter | solution.py:556
  287.0 4.3 collective-permute-start.1
  289.7 1.5 collective-permute-start
  293.4 517.2 %reduce-scatter.17.cloned.1.call-start = ((), (), s32[]{:S(2)}) async-start(), calls=%async_computation.16 | async-start | bytes 2506752 | tf_op jit(solution)/shard_map/reduce_scatter | solution.py:556
  293.6 2.1 collective-permute-start.4
  294.0 1.6 collective-permute-start.5
  297.9 646.0 %reduce-scatter.15.cloned.1.call-start = ((), (), s32[]{:S(2)}) async-start(), calls=%async_computation.15 | async-start | bytes 2506752 | tf_op jit(solution)/shard_map/reduce_scatter | solution.py:556
  297.9 2.6 collective-permute-start.3
  298.8 1.6 collective-permute-start.2
  304.2 770.5 %reduce-scatter.11.cloned.1.call-start = ((), (), s32[]{:S(2)}) async-start(), calls=%async_computation.13 | async-start | bytes 1880064 | tf_op jit(solution)/shard_map/reduce_scatter | solution.py:556
  417.6 789.0 %all-reduce.7.cloned.1.call-start = ((), (), s32[]{:S(2)}) async-start(), calls=%async_computation.12 | async-start | bytes 786432 | tf_op jit(solution)/shard_map/psum | solution.py:594
  421.1 131.9 %copy-start.7 = (bf16[128,768]{1,0:T(8,128)(2,1)}, bf16[128,768]{1,0:T(8,128)(2,1)S(1)}, u32[]{:S(2)}) copy-start(bf16[128,768]{1,0:T(8,128)(2,1)S(1)} %fusion.15) | copy-start | bytes 589828
  422.2 130.8 %copy-start.10 = (f32[128,768]{1,0:T(8,128)S(1)}, f32[128,768]{1,0:T(8,128)}, u32[]{:S(2)}) copy-start(f32[128,768]{1,0:T(8,128)} %get-tuple-element.115) | copy-start | bytes 1179652
  422.2 130.9 %copy-start.30 = (f32[128]{0:T(128)S(1)}, f32[128]{0:T(128)}, u32[]{:S(2)}) copy-start(f32[128]{0:T(128)} %copy-done.29) | copy-start | bytes 1540
  422.2 130.9 %copy-start.34 = (f32[128]{0:T(128)S(1)}, f32[128]{0:T(128)}, u32[]{:S(2)}) copy-start(f32[128]{0:T(128)} %copy-done.33) | copy-start | bytes 1540
  422.2 131.1 %copy-start.41 = (s32[1,128]{1,0:T(1,128)S(1)}, s32[1,128]{1,0:T(1,128)}, u32[]{:S(2)}) copy-start(s32[1,128]{1,0:T(1,128)} %param.22) | copy-start | bytes 1540
  553.1 392.4 %copy-start.24 = (f32[768]{0:T(1024)S(1)}, f32[768]{0:T(1024)}, u32[]{:S(2)}) copy-start(f32[768]{0:T(1024)} %get-tuple-element.96) | copy-start | bytes 9220
  553.1 392.4 %copy-start.25 = (f32[768]{0:T(1024)S(1)}, f32[768]{0:T(1024)}, u32[]{:S(2)}) copy-start(f32[768]{0:T(1024)} %get-tuple-element.102) | copy-start | bytes 9220
  553.1 392.4 %copy-start.26 = (f32[32,128]{1,0:T(8,128)S(1)}, f32[32,128]{1,0:T(8,128)}, u32[]{:S(2)}) copy-start(f32[32,128]{1,0:T(8,128)} %get-tuple-element.31) | copy-start | bytes 49156
  553.1 655.3 %copy-start.1 = (bf16[128,768]{1,0:T(8,128)(2,1)S(1)}, bf16[128,768]{1,0:T(8,128)(2,1)}, u32[]{:S(2)}) copy-start(bf16[128,768]{1,0:T(8,128)(2,1)} %param.25) | copy-start | bytes 589828
  553.3 655.1 %copy-start.11 = (f32[128,768]{1,0:T(8,128)}, f32[128,768]{1,0:T(8,128)S(1)}, u32[]{:S(2)}) copy-start(f32[128,768]{1,0:T(8,128)S(1)} %multiply_add_fusion.2) | copy-start | bytes 1179652
  (32 other events, 166.4 us)
Sparse Core Ops, SparseCore 0:
  11.3 15.2 all-gather.6
  30.0 69.3 all-gather.8
  100.9 7.7 all-gather.10
  110.1 15.5 all-gather.12
  127.1 15.6 all-gather.14
  275.4 138.2 reduce-scatter.18
  419.5 131.8 reduce-scatter.8
  556.7 121.4 reduce-scatter.12
  683.2 127.3 reduce-scatter.16
  816.1 127.6 reduce-scatter.14
  948.7 125.8 reduce-scatter.10
  1080.3 126.2 all-reduce.6

commit v2 on v1

--- a/solution.py
+++ b/solution.py
@@ -183,18 +183,19 @@
 def bwd_kernel(
     head_dim, lo_ref, hi_ref, p_ref, rl_ref, q_ref, do_ref, o_ref, k_ref, vt_ref, qpos_ref, kpos_ref,
     cen_ref, amp_ref, lnorm_ref, wp_ref, dq_ref, dkt_ref, dvt_ref, m0_ref, sums_ref,
-    qext, doexp, doext, delta, dqacc, glow, dist, kern, gk,
+    qext, doexp, doext, delta, dqacc, glow, dist, kern, gk, dkt_acc, dvt_acc,
 ):
     block = pl.program_id(0)
     lo, hi = lo_ref[block], hi_ref[block]
     groups = q_ref.shape[1] // GW
     rows = QB * HG
+    scale = head_dim ** (-0.5)
     mask = head_mask(head_dim)
 
     @pl.when(block == 0)
     def _():
-        dkt_ref[...] = jnp.zeros(dkt_ref.shape, f32)
-        dvt_ref[...] = jnp.zeros(dvt_ref.shape, f32)
+        dkt_acc[...] = jnp.zeros(dkt_acc.shape, f32)
+        dvt_acc[...] = jnp.zeros(dvt_acc.shape, f32)
         m0_ref[...] = jnp.zeros(m0_ref.shape, f32)
         sums_ref[...] = jnp.zeros(sums_ref.shape, f32)
 
@@ -212,6 +213,7 @@
         dqacc[g] = jnp.zeros((rows, GW), f32)
 
     def one_tile(tile, carry):
+        keys = pl.ds(pl.multiple_of(tile * TILE, TILE), TILE)
         dist[...] = tile_distance(qpos_ref, kpos_ref, tile)
         for pair in range(groups // 2):
             grads = []
@@ -224,8 +226,8 @@
                 grads.append(gl)
                 gl_low = gl.astype(bf16)
                 dqacc[g] += jnp.dot(gl_low, k_ref[tile, :, lanes], preferred_element_type=f32)
-                dkt_ref[tile, lanes, :] += jnp.dot(qext[g], gl_low, preferred_element_type=f32)
-                dvt_ref[tile, lanes, :] += jnp.dot(doext[g], low, preferred_element_type=f32)
+                dkt_acc[lanes, keys] += jnp.dot(qext[g], gl_low, preferred_element_type=f32)
+                dvt_acc[lanes, keys] += jnp.dot(doext[g], low, preferred_element_type=f32)
             for i in range(QB):
                 at = slice(i * HG, (i + 1) * HG)
                 glow[pair * 16 : (pair + 1) * 16, i * TILE : (i + 1) * TILE] = jnp.concatenate(
@@ -264,7 +266,12 @@
 
     lax.fori_loop(lo, hi, one_tile, 0)
     for g in range(groups):
-        dq_ref[:, g * GW : (g + 1) * GW] = collapse(dqacc[g], mask)
+        dq_ref[:, g * GW : (g + 1) * GW] = (collapse(dqacc[g], mask) * scale).astype(bf16)
+
+    @pl.when(block == pl.num_programs(0) - 1)
+    def _():
+        dkt_ref[...] = (dkt_acc[...] * scale).astype(bf16)
+        dvt_ref[...] = dvt_acc[...].astype(bf16)
 
 
 def whole(shape):
@@ -320,6 +327,9 @@
             jax.ShapeDtypeStruct((blocks * groups * rows, TILE), f32),
         ],
         compiler_params=pltpu.CompilerParams(vmem_limit_bytes=60 << 20),
+        cost_estimate=pl.CostEstimate(
+            flops=30_000_000_000, bytes_accessed=40_000_000, transcendentals=200_000_000
+        ),
         name="attend",
     )(lo, hi, q, kt, v, qpos, kpos, qid, kid, cen, amp, lnorm, wpt)
 
@@ -354,8 +364,8 @@
             ],
             out_specs=[
                 pl.BlockSpec((QB, wide), by_block),
-                whole(vt.shape),
-                whole(vt.shape),
+                whole((wide, tiles * TILE)),
+                whole((wide, tiles * TILE)),
                 whole((heads, kernels)),
                 whole((3, kernels, TILE)),
             ],
@@ -369,18 +379,320 @@
                 pltpu.VMEM((QB, TILE), f32),
                 pltpu.VMEM((kernels, QB * TILE), bf16),
                 pltpu.VMEM((kernels, QB * TILE), f32),
+                pltpu.VMEM((wide, tiles * TILE), f32),
+                pltpu.VMEM((wide, tiles * TILE), f32),
             ],
         ),
         out_shape=[
-            jax.ShapeDtypeStruct(q.shape, f32),
-            jax.ShapeDtypeStruct(vt.shape, f32),
-            jax.ShapeDtypeStruct(vt.shape, f32),
+            jax.ShapeDtypeStruct(q.shape, bf16),
+            jax.ShapeDtypeStruct((wide, tiles * TILE), bf16),
+            jax.ShapeDtypeStruct((wide, tiles * TILE), bf16),
             jax.ShapeDtypeStruct((heads, kernels), f32),
             jax.ShapeDtypeStruct((3, kernels, TILE), f32),
         ],
-        compiler_params=pltpu.CompilerParams(vmem_limit_bytes=60 << 20),
+        compiler_params=pltpu.CompilerParams(vmem_limit_bytes=62 << 20),
+        cost_estimate=pl.CostEstimate(
+            flops=60_000_000_000, bytes_accessed=60_000_000, transcendentals=200_000_000
+        ),
         name="attend_back",
     )(lo, hi, p, rl, q, do, o, k, vt, qpos, kpos, cen, amp, lnorm, wp)
+
+
+MESH = pl.DeviceIdType.MESH
+INNER = 4
+
+
+def places():
+    row, core = lax.axis_index("row"), lax.axis_index("wt")
+    outer, inner = row // INNER, row % INNER
+    return row, core, outer, inner
+
+
+def plane_mates(inner):
+    y, x = inner // 2, inner % 2
+    return (y * 2 + (1 - x), (1 - y) * 2 + x, (1 - y) * 2 + (1 - x))
+
+
+def greet(targets):
+    barrier = pltpu.get_barrier_semaphore()
+    for target in targets:
+        pl.semaphore_signal(barrier, inc=1, device_id=target, device_id_type=MESH)
+    pl.semaphore_wait(barrier, len(targets))
+
+
+def remote(src, dst, send_sem, recv_sem, target):
+    return pltpu.make_async_remote_copy(
+        src_ref=src, dst_ref=dst, send_sem=send_sem, recv_sem=recv_sem,
+        device_id=target, device_id_type=MESH,
+    )
+
+
+def gather_kernel(outers, x_ref, c_ref, xo_ref, co_ref, sends, gets, sends_c, gets_c):
+    row, core, outer, inner = places()
+    mates = plane_mates(inner)
+    far = [(outer + step) % outers for step in range(1, outers)]
+    plane = [(outer * INNER + mate, core) for mate in mates]
+    column = [(other * INNER + inner, core) for other in far]
+    greet(plane + column)
+    started = []
+
+    def send(src, src_c, slot, target):
+        at = len(started) // 2
+        for copy in (
+            remote(src, xo_ref.at[slot], sends.at[at], gets.at[slot], target),
+            remote(src_c, co_ref.at[slot], sends_c.at[at], gets_c.at[slot], target),
+        ):
+            copy.start()
+            started.append(copy)
+
+    for target in column:
+        send(x_ref, c_ref, row, target)
+    for target in plane:
+        send(x_ref, c_ref, row, target)
+    xo_ref[row] = x_ref[...]
+    co_ref[row] = c_ref[...]
+
+    def arrived(slot):
+        remote(x_ref, xo_ref.at[slot], sends.at[0], gets.at[slot], (row, core)).wait_recv()
+        remote(c_ref, co_ref.at[slot], sends_c.at[0], gets_c.at[slot], (row, core)).wait_recv()
+
+    for step in range(1, outers):
+        slot = ((outer + outers - step) % outers) * INNER + inner
+        arrived(slot)
+        for target in plane:
+            send(xo_ref.at[slot], co_ref.at[slot], slot, target)
+    for mate in mates:
+        for step in range(outers):
+            arrived(((outer + outers - step) % outers) * INNER + mate)
+    for copy in started:
+        copy.wait_send()
+
+
+def gather_rows(x, c, rows):
+    outers = rows // INNER
+    count = (outers - 1) + 3 * outers
+    vmem = pl.BlockSpec(memory_space=pltpu.VMEM)
+    return pl.pallas_call(
+        functools.partial(gather_kernel, outers),
+        out_shape=[
+            jax.ShapeDtypeStruct((rows,) + x.shape, x.dtype),
+            jax.ShapeDtypeStruct((rows,) + c.shape, c.dtype),
+        ],
+        in_specs=[vmem, vmem],
+        out_specs=[vmem, vmem],
+        scratch_shapes=[
+            pltpu.SemaphoreType.DMA((count,)),
+            pltpu.SemaphoreType.DMA((rows,)),
+            pltpu.SemaphoreType.DMA((count,)),
+            pltpu.SemaphoreType.DMA((rows,)),
+        ],
+        compiler_params=pltpu.CompilerParams(
+            collective_id=0, has_side_effects=True, vmem_limit_bytes=40 << 20
+        ),
+        name="gather_rows",
+    )(x, c)
+
+
+def finish_kernel(outers, part_width, dkt_ref, dvt_ref, dq_ref, every_ref, own_ref, wq_ref, wk_ref, wv_ref, xo_ref, wo_ref,
+                  xs, xa, xm, xb, wp, wi, wa, wm, wb, w0_sems, a_send, a_recv, b_send, b_recv):
+    row, core, outer, inner = places()
+    mates = plane_mates(inner)
+    count, width = own_ref.shape
+    half = width // 2
+    used = part_width * 8
+    rows_each = wo_ref.shape[0]
+    plane = [(outer * INNER + mate, core) for mate in mates]
+    far = [(outer + step) % outers for step in range(1, outers)]
+    column = [(other * INNER + inner, core) for other in far]
+    order = far + [outer]
+    greet(plane + column + [(row, 1 - core)])
+    started = []
+
+    def grad_chunk(slot):
+        at = pl.ds(pl.multiple_of(slot * count, count), count)
+        flipped = jnp.dot(wk_ref[...], dkt_ref[:, at], preferred_element_type=f32)
+        flipped += jnp.dot(wv_ref[...], dvt_ref[:, at], preferred_element_type=f32)
+        return jnp.transpose(flipped)
+
+    def begin(copy):
+        copy.start()
+        started.append(copy)
+
+    def to_mate(which, at, o, p, src, dst):
+        return remote(src, dst, a_send.at[which, p, at], a_recv.at[which, p, o], plane[p])
+
+    for at, o in enumerate(order):
+        for p in range(3):
+            xs[o, mates[p]] = grad_chunk(o * INNER + mates[p]).astype(bf16)
+            begin(to_mate(0, at, o, p, xs.at[o, mates[p]], xa.at[p, o]))
+    for o in order:
+        xs[o, inner] = grad_chunk(o * INNER + inner).astype(bf16)
+
+    def key_part(index, carry):
+        g = index
+        here = pl.ds(pl.multiple_of(g * GW, GW), used)
+        there = pl.ds(pl.multiple_of(g * used, 16), used)
+        wp[there, :] = lax.dot_general(
+            dq_ref[:, pl.ds(pl.multiple_of(g * GW, GW), GW)], own_ref[...], (((0,), (0,)), ((), ())),
+            preferred_element_type=f32,
+        )[:used, :].astype(bf16)
+        there = pl.ds(pl.multiple_of(width + g * used, 16), used)
+        wp[there, :] = jnp.dot(dkt_ref[here, :], every_ref[...], preferred_element_type=f32).astype(bf16)
+        there = pl.ds(pl.multiple_of(2 * width + g * used, 16), used)
+        wp[there, :] = jnp.dot(dvt_ref[here, :], every_ref[...], preferred_element_type=f32).astype(bf16)
+        return carry
+
+    lax.fori_loop(0, width // used, key_part, 0)
+    other_lanes = pl.ds(pl.multiple_of((1 - core) * half, 128), half)
+    own_lanes = pl.ds(pl.multiple_of(core * half, 128), half)
+    halves = remote(wp.at[:, other_lanes], wi, w0_sems.at[0], w0_sems.at[1], (row, 1 - core))
+    halves.start()
+
+    def plane_sum(which, own, got, o):
+        total = own.astype(f32)
+        for p in range(3):
+            to_mate(which, 0, o, p, got.at[p, o], got.at[p, o]).wait_recv()
+            total = total + got[p, o].astype(f32)
+        return total
+
+    def to_far(which, step, stage, last):
+        return remote(
+            stage.at[step], last.at[step], b_send.at[which, step], b_recv.at[which, step], column[step]
+        )
+
+    for step, o in enumerate(far):
+        xm[step] = plane_sum(0, xs[o, inner], xa, o).astype(bf16)
+        begin(to_far(0, step, xm, xb))
+    halves.wait_recv()
+    wi[...] = (wp[:, own_lanes].astype(f32) + wi[...].astype(f32)).astype(bf16)
+
+    def w_rows(slot):
+        return pl.ds(pl.multiple_of(slot * rows_each, 16), rows_each)
+
+    for at, o in enumerate(order):
+        for p in range(3):
+            begin(to_mate(1, at, o, p, wi.at[w_rows(o * INNER + mates[p])], wa.at[p, o]))
+    flipped = lax.dot_general(
+        wq_ref[...], dq_ref[...], (((1,), (1,)), ((), ())), preferred_element_type=f32
+    )
+    total = plane_sum(0, xs[outer, inner], xa, outer) + jnp.transpose(flipped)
+    for step in range(outers - 1):
+        to_far(0, step, xm, xb).wait_recv()
+        total = total + xb[step].astype(f32)
+    xo_ref[...] = total
+    for step, o in enumerate(far):
+        wm[step] = plane_sum(1, wi[w_rows(o * INNER + inner), :], wa, o).astype(bf16)
+        begin(to_far(1, step, wm, wb))
+    total = plane_sum(1, wi[w_rows(outer * INNER + inner), :], wa, outer)
+    for step in range(outers - 1):
+        to_far(1, step, wm, wb).wait_recv()
+        total = total + wb[step].astype(f32)
+    wo_ref[...] = total
+    halves.wait_send()
+    for copy in started:
+        copy.wait_send()
+
+
+def finish_rows(dkt, dvt, dq, every, own, w_q, w_k, w_v, rows, head_dim):
+    outers = rows // INNER
+    count, width = own.shape
+    each = 3 * width // rows
+    half = width // 2
+    vmem = pl.BlockSpec(memory_space=pltpu.VMEM)
+    return pl.pallas_call(
+        functools.partial(finish_kernel, outers, head_dim),
+        out_shape=[
+            jax.ShapeDtypeStruct((count, width), f32),
+            jax.ShapeDtypeStruct((each, half), f32),
+        ],
+        in_specs=[vmem] * 8,
+        out_specs=[vmem] * 2,
+        scratch_shapes=[
+            pltpu.VMEM((outers, INNER, count, width), bf16),
+            pltpu.VMEM((3, outers, count, width), bf16),
+            pltpu.VMEM((outers - 1, count, width), bf16),
+            pltpu.VMEM((outers - 1, count, width), bf16),
+            pltpu.VMEM((3 * width, width), bf16),
+            pltpu.VMEM((3 * width, half), bf16),
+            pltpu.VMEM((3, outers, each, half), bf16),
+            pltpu.VMEM((outers - 1, each, half), bf16),
+            pltpu.VMEM((outers - 1, each, half), bf16),
+            pltpu.SemaphoreType.DMA((2,)),
+            pltpu.SemaphoreType.DMA((2, 3, outers)),
+            pltpu.SemaphoreType.DMA((2, 3, outers)),
+            pltpu.SemaphoreType.DMA((2, outers - 1)),
+            pltpu.SemaphoreType.DMA((2, outers - 1)),
+        ],
+        compiler_params=pltpu.CompilerParams(
+            collective_id=1, has_side_effects=True, vmem_limit_bytes=60 << 20
+        ),
+        name="finish_rows",
+    )(dkt, dvt, dq, every, own, w_q, w_k, w_v)
+
+
+def total_kernel(count, x_ref, out_ref, got, s1, r1, s2, r2):
+    row, core = lax.axis_index("row"), lax.axis_index("wt")
+    me = row * 2 + core
+    barrier = pltpu.get_barrier_semaphore()
+
+    def place(step):
+        other = (me + step) % count
+        return other, (other // 2, other % 2)
+
+    def hello(step, carry):
+        pl.semaphore_signal(barrier, inc=1, device_id=place(step)[1], device_id_type=MESH)
+        return carry
+
+    lax.fori_loop(1, count, hello, 0)
+    pl.semaphore_wait(barrier, count - 1)
+
+    def first(step):
+        other, target = place(step)
+        return remote(x_ref.at[other], got.at[step], s1.at[step], r1.at[step], target)
+
+    def second(step):
+        return remote(out_ref.at[me], out_ref.at[me], s2.at[step], r2.at[step], place(step)[1])
+
+    def from_other(step):
+        other = (me + count - step) % count
+        return remote(out_ref.at[me], out_ref.at[other], s2.at[step], r2.at[step], place(step)[1])
+
+    def start_first(step, carry):
+        first(step).start()
+        return carry
+
+    def add(step, total):
+        first(step).wait_recv()
+        return total + got[step]
+
+    def start_second(step, carry):
+        second(step).start()
+        return carry
+
+    def end(step, carry):
+        from_other(step).wait_recv()
+        first(step).wait_send()
+        second(step).wait_send()
+        return carry
+
+    lax.fori_loop(1, count, start_first, 0)
+    out_ref[me] = lax.fori_loop(1, count, add, x_ref[me])
+    lax.fori_loop(1, count, start_second, 0)
+    lax.fori_loop(1, count, end, 0)
+
+
+def total_over_all(x):
+    count = x.shape[0]
+    vmem = pl.BlockSpec(memory_space=pltpu.VMEM)
+    return pl.pallas_call(
+        functools.partial(total_kernel, count),
+        out_shape=jax.ShapeDtypeStruct(x.shape, f32),
+        in_specs=[vmem],
+        out_specs=vmem,
+        scratch_shapes=[pltpu.VMEM(x.shape, f32)] + [pltpu.SemaphoreType.DMA((count,))] * 4,
+        compiler_params=pltpu.CompilerParams(collective_id=2, has_side_effects=True),
+        name="total_over_all",
+    )(x)
 
 
 def on_device(
@@ -482,8 +794,15 @@
     )
     normed_one, inverse_one = norm_parts(base_rows)
     normed_in = (normed_one * gain_one + shift_one).astype(bf16)
-    every = fetch(normed_in, 0)
-    positions = fetch(coords[:, 0, :], 1).astype(f32)
+    if covers:
+        low_pos = jnp.pad(coords[:, 0, :], ((0, 13), (0, 0)))
+        every, every_pos = gather_rows(normed_in, low_pos, row_size)
+        every = every.reshape(key_count, model_width)
+        kpos = every_pos[:, :3, :].astype(f32)
+    else:
+        every = fetch(normed_in, 0)
+        positions = fetch(coords[:, 0, :], 1).astype(f32)
+        kpos = jnp.swapaxes(positions.reshape(3, tiles, TILE), 0, 1)
 
     queries = jnp.dot(normed_in, w_q, preferred_element_type=f32).astype(bf16)
     keys = jnp.dot(every, w_k, preferred_element_type=f32).astype(bf16)
@@ -494,7 +813,6 @@
     keys_t = jnp.swapaxes(keys, 1, 2)
     values_t = jnp.swapaxes(values, 1, 2)
     qpos = jnp.transpose(coords[:, 0, :].astype(f32))
-    kpos = jnp.swapaxes(positions.reshape(3, tiles, TILE), 0, 1)
     qid = own_ids[:, None]
     kid = key_ids.reshape(tiles, 1, TILE)
     steep = math.sqrt(0.5 * LOG2E)
@@ -547,36 +865,104 @@
         half = x.shape[1] // 2
         return jnp.where(my_core == 0, x[:, half:], x[:, :half])
 
-    def weight_grad(left, right):
+    def both_cores(left, right):
         lefts = jnp.concatenate([my_half(left), swap_cores(other_half(left))], axis=0)
         rights = jnp.concatenate([right, swap_cores(right)], axis=0)
-        return cross_rows(lefts, rights).astype(bf16)
+        return lefts, rights
+
+    def weight_grads(pairs):
+        pieces = []
+        for left, right in pairs:
+            lefts, rights = both_cores(left, right)
+            for at in range(0, lefts.shape[1], model_width // 2):
+                piece = cross_rows(rights, lefts[:, at : at + model_width // 2])
+                pieces.append(piece.astype(bf16).reshape(row_size, -1, model_width // 2))
+        return jnp.concatenate(pieces, axis=1)
+
+    ffn_grads = weight_grads(
+        [(ffn_in, grad_hidden_low), (att_low, grad_after_low), (activated, grad_sum_low)]
+    )
+
+    def split_grads(total):
+        up, out = w_up.shape[1] // row_size, w_out.shape[1] // row_size
+        down = total[up + out :].reshape(-1, out, model_width // 2)
+        return (
+            jnp.transpose(total[:up]),
+            jnp.transpose(total[up : up + out]),
+            jnp.transpose(jnp.concatenate([x for x in down], axis=1)),
+        )
+
+    outer, inner = my_index // INNER, my_index % INNER
+    outers = row_size // INNER
+
+    def by_plane(x, which):
+        return lax.dynamic_index_in_dim(x.reshape((outers, INNER) + x.shape[1:]), which, 1, False)
+
+    def to_planes():
+        arrived = []
+        for flip in (1, 2, 3):
+            pairs = [(r, r ^ flip) for r in range(row_size)]
+            arrived.append(lax.ppermute(by_plane(ffn_grads, inner ^ flip), "row", pairs))
+        return arrived
+
+    def plane_sums(arrived):
+        total = by_plane(ffn_grads, inner).astype(f32)
+        for some in arrived:
+            total = total + some.astype(f32)
+        own = lax.dynamic_index_in_dim(total, outer, 0, False)
+        others = [
+            lax.dynamic_index_in_dim(total, (outer + step) % outers, 0, False).astype(bf16)
+            for step in range(1, outers)
+        ]
+        return own, others
+
+    def to_columns(others):
+        arrived = []
+        for step in range(1, outers):
+            pairs = [
+                (r, ((r // INNER + step) % outers) * INNER + r % INNER) for r in range(row_size)
+            ]
+            arrived.append(lax.ppermute(others[step - 1], "row", pairs))
+        return arrived
 
     def over_rows(x):
-        return lax.psum_scatter(x, "row", scatter_dimension=1, tiled=True).astype(f32)
-
-    w_down_grad = over_rows(weight_grad(activated, grad_sum_low))
-    w_up_grad = over_rows(weight_grad(ffn_in, grad_hidden_low))
-    w_out_grad = over_rows(weight_grad(att_low, grad_after_low))
+        return jnp.transpose(
+            lax.psum_scatter(x, "row", scatter_dimension=0, tiled=False).astype(f32)
+        )
+
+    do_wide = padded(grad_att_low, 1)
+    do_wide, ffn_grads = lax.optimization_barrier((do_wide, ffn_grads))
+    if covers:
+        arrived = to_planes()
+    else:
+        summed = lax.psum_scatter(ffn_grads, "row", scatter_dimension=0, tiled=False).astype(f32)
 
     dq, dkt, dvt, pair_t, kernel_sums = attention_backward(
-        lo, hi, probs, inverse_total, queries, padded(grad_att_low, 1), att_wide, keys, values_t,
+        lo, hi, probs, inverse_total, queries, do_wide, att_wide, keys, values_t,
         qpos, kpos, cen, amp, lnorm, w_pair, head_dim,
     )
-    query_grad = (dq * score_scale).astype(bf16)
-    key_grad = (jnp.swapaxes(dkt, 1, 2).reshape(key_count, wide) * score_scale).astype(bf16)
-    value_grad = jnp.swapaxes(dvt, 1, 2).reshape(key_count, wide).astype(bf16)
-    grad_every = along_rows(key_grad, w_k) + along_rows(value_grad, w_v)
-    grad_normed_in = along_rows(query_grad, w_q) + send_back(grad_every)
-    qkv_grad_w = jnp.concatenate(
-        [
-            unpadded(cross_rows(normed_in, query_grad), 1),
-            unpadded(cross_rows(every, key_grad), 1),
-            unpadded(cross_rows(every, value_grad), 1),
-        ],
-        axis=1,
-    ).astype(bf16)
-    w_qkv_grad = over_rows(lax.psum_scatter(qkv_grad_w, "wt", scatter_dimension=0, tiled=True))
+    if covers:
+        dq, arrived = lax.optimization_barrier((dq, arrived))
+        own_sum, others = plane_sums(arrived)
+        dq, others = lax.optimization_barrier((dq, others))
+        far_sums = to_columns(others)
+        grad_normed_in, w_qkv_grad_t = finish_rows(
+            dkt, dvt, dq, every, normed_in, w_q, w_k, w_v, row_size, head_dim
+        )
+        grad_normed_in, far_sums = lax.optimization_barrier((grad_normed_in, far_sums))
+        summed = own_sum + sum(x.astype(f32) for x in far_sums)
+        w_qkv_grad = jnp.transpose(w_qkv_grad_t)
+    else:
+        key_grad, value_grad = jnp.transpose(dkt), jnp.transpose(dvt)
+        grad_every = along_rows(key_grad, w_k) + along_rows(value_grad, w_v)
+        grad_normed_in = along_rows(dq, w_q) + send_back(grad_every)
+        parts = [(normed_in, dq), (every, key_grad), (every, value_grad)]
+        whole_grad = jnp.concatenate(
+            [unpadded(cross_rows(right, left), 0) for left, right in parts], axis=0
+        ).astype(bf16)
+        half_grad = lax.psum_scatter(whole_grad, "wt", scatter_dimension=1, tiled=True)
+        w_qkv_grad = over_rows(half_grad.reshape(row_size, -1, half_grad.shape[1]))
+    w_up_grad, w_out_grad, w_down_grad = split_grads(summed)
     grad_norm_one, grad_gain_one, grad_shift_one = norm_back(
         grad_normed_in, normed_one, inverse_one, gain_one
     )
@@ -591,20 +977,29 @@
     sums = jnp.sum(kernel_sums, axis=2)
     center_part = sums[1] / (steep * widths)
     width_part = (sums[2] / (steep * steep) - sums[0]) / widths
-    small_sums = lax.psum(
-        (
-            grad_table,
-            grad_gain_one,
-            grad_shift_one,
-            center_part,
-            width_part,
-            jnp.transpose(pair_t),
-            grad_gain_two,
-            grad_shift_two,
-            grad_force,
-        ),
-        ("row", "wt"),
-    )
+    small = (
+        grad_table,
+        grad_gain_one,
+        grad_shift_one,
+        center_part,
+        width_part,
+        jnp.transpose(pair_t),
+        grad_gain_two,
+        grad_shift_two,
+        grad_force,
+    )
+    if covers:
+        flat = jnp.concatenate([x.reshape(-1) for x in small])
+        devices = row_size * lax.axis_size("wt")
+        piece = -(-flat.shape[0] // (devices * 8 * 128)) * 128
+        flat = jnp.pad(flat, (0, devices * 8 * piece - flat.shape[0]))
+        flat = total_over_all(flat.reshape(devices, 8, piece)).reshape(-1)
+        small_sums, at = [], 0
+        for x in small:
+            small_sums.append(flat[at : at + x.size].reshape(x.shape))
+            at += x.size
+    else:
+        small_sums = lax.psum(small, ("row", "wt"))
     return (
         out_low[None],
         force_rows[:, None, :],

time: 1220 us -> 476 us (0.39)
  waiting for transfers between devices: 877 us -> 10.8 us
  Pallas kernels: 48.2 us -> 205 us
  starting transfers between devices: 2.77 us -> 118 us
  blocking collectives: 84.2 us -> 0 us
  matrix products: 73.7 us -> 43.6 us
  local copies, waits for them, and re-layouts: 83.6 us -> 58.5 us
    reduce_scatter x5 -> x0, waiting for transfers between devices: 603 us -> none  [the longest x4 474 us: over_rows(): lax.psum_scatter(x, 'row', scatter_dimension=1, tiled=True).astype(f32)]
    pallas_call x0 -> x3, Pallas kernels: none -> 138 us  [the longest x1 66.5 us: finish_rows(): pl.pallas_call(functools.partial(finish_kernel, outers, head_dim), out_sh...]
    psum x1 -> x0, waiting for transfers between devices: 130 us -> none  [on_device(): lax.psum((grad_table, grad_gain_one, grad_shift_one, center_part, width_p...]
    ppermute x0 -> x6, starting transfers between devices: none -> 115 us  [the longest x3 108 us: to_columns(): arrived.append(lax.ppermute(others[step - 1], 'row', pairs))]
    unnamed x13 -> x4, waiting for transfers between devices: 111 us -> 1.41 us
    all_gather x1 -> x0, blocking collectives: 42.4 us -> none  [fetch(): return lax.all_gather(x, 'row', axis=axis, tiled=True)]
    psum x1 -> x0, blocking collectives: 41.8 us -> none  [on_device(): lax.psum((grad_table, grad_gain_one, grad_shift_one, center_part, width_p...]
    all_gather x1 -> x0, waiting for transfers between devices: 29.1 us -> none  [fetch(): return lax.all_gather(x, 'row', axis=axis, tiled=True)]
  transfers between devices with their start and end apart: 18 -> 16, of which waited for: 12 -> 2; matrix products, arithmetic and copies ran while one was open for 8% -> 18% of each run, Pallas kernels for 1% -> 38%
where the time goes in v2:
time: 476 us; the launch traced here: 470 us
  Pallas kernels  205 us (43%)
  starting transfers between devices  118 us (25%)
  local copies, waits for them, and re-layouts  58.5 us (12%)
  matrix products  43.6 us (9%)
  other arithmetic  18 us (4%)
  between operations  15.8 us (3%)
  waiting for transfers between devices  10.8 us (2%)
    ppermute x3, starting transfers between devices, to_columns(): arrived.append(lax.ppermute(others[step - 1], 'row', pairs))  108 us
    pallas_call x1, Pallas kernels, finish_rows(): pl.pallas_call(functools.partial(finish_kernel, outers, head_dim), out_sh...  66.5 us
    pallas_call x1, Pallas kernels, attention_backward(): pl.pallas_call(functools.partial(bwd_kernel, head_dim), grid_spec=pltpu.P...  48.5 us
    pallas_call x1, Pallas kernels, gather_rows(): pl.pallas_call(functools.partial(gather_kernel, outers), out_shape=[jax.S...  43.3 us
    pallas_call x1, Pallas kernels, total_over_all(): pl.pallas_call(functools.partial(total_kernel, count), out_shape=jax.Shap...  27.9 us
    pallas_call x1, Pallas kernels, attention_forward(): pl.pallas_call(functools.partial(fwd_kernel, head_dim), grid_spec=pltpu.P...  19.1 us
    unnamed x125, local copies, waits for them, and re-layouts  14.9 us
    dot_general x4, matrix products, along_rows(): lax.dot_general(left_side, right_side, (((1,), (1,)), ((), ())), preferre...  11.1 us
  transfers between devices with their start and end apart: 16, of which 2 were waited for; matrix products, arithmetic and copies ran while one was open for 18% of the time, Pallas kernels for 38%

profile of v2, /device:TPU:0, one launch (start us, length us, event | category | flops | bytes accessed | tf_op | source)
XLA Modules:
  0.0 469.7 jit_solution(945912131035587248)
XLA Ops:
  7.2 3.9 copy.65
  19.1 43.3 %gather_rows.1 = (bf16[16,128,768]{2,1,0:T(8,128)(2,1)S(1)}, bf16[16,16,128]{2,1,0:T(8,128)(2,1)S(1)}) custom-call(bf16[128,768]{1,0:T(8,128)(2,1)S(1)} %add_convert_fusion.1.x_ref.own_ref, bf16[16,128]{1,0:T(8,128)(2,1)S(1)} %pad.23.clone.c_ref), custom_call_target="tpu_custom_call" | custom-call | tf_op jit(solution)/shard_map/gather_rows/pallas_call | solution.py:475
  68.0 4.1 fusion.50
  74.8 2.6 copy.83.wq_ref
  77.4 2.6 pad.24
  79.9 2.6 copy.84.wk_ref
  82.5 6.5 %convolution_convert_fusion.2 = bf16[2048,1024]{1,0:T(8,128)(2,1)} fusion(bf16[2048,768]{1,0:T(8,128)(2,1)S(1)} %bitcast.109, bf16[768,1024]{0,1:T(8,128)(2,1)} %bitcast.118), kind=kOutput, calls=%fused_computation.2 | convolution fusion | flops 3223322624 | bytes 8912896 | tf_op jit(solution)/shard_map/dot_general | solution.py:808
  90.3 5.0 %convolution_convert_fusion.1 = bf16[2048,1024]{1,0:T(8,128)(2,1)} fusion(bf16[2048,768]{1,0:T(8,128)(2,1)S(1)} %bitcast.110, bf16[768,1024]{0,1:T(8,128)(2,1)S(1)} %bitcast.119), kind=kOutput, calls=%fused_computation.1 | convolution fusion | flops 3223322624 | bytes 8912896 | tf_op jit(solution)/shard_map/dot_general | solution.py:809
  95.4 2.6 copy.85.wv_ref
  98.0 6.4 %copy.71.kt_ref = bf16[16,1024,128]{2,1,0:T(8,128)(2,1)} copy(bf16[16,1024,128]{1,2,0:T(8,128)(2,1)} %bitcast.124) | data formatting | bytes 8388608 | tf_op jit(solution)/shard_map/transpose | solution.py:813
  104.4 6.4 %copy.78 = bf16[16,128,1024]{1,2,0:T(8,128)(2,1)} copy(bf16[16,128,1024]{2,1,0:T(8,128)(2,1)} %bitcast.127) | data formatting | bytes 8388608 | tf_op jit(solution)/shard_map/reshape | solution.py:811
  112.9 19.1 %attend.1 = (bf16[4,16,1024,128]{3,2,1,0:T(8,128)(2,1)}, f32[128,1024]{1,0:T(8,128)}, f32[4096,128]{1,0:T(8,128)}) custom-call(s32[4]{0:T(128)} %get-tuple-element.170.lo_ref, s32[4]{0:T(128)} %get-tuple-element.169.hi_ref, bf16[128,1024]{1,0:T(8,128)(2,1)} %convolution_convert_fusion.9.q_ref, bf16[16,1024,128]{2,1,0:T(8,128)(2,1)} %copy.71.kt_ref, ...), custom_call_target="tpu_custom_call" | custom-call | flops 30000001024 | bytes 40000000 | tf_op jit(solution)/shard_map/attend/pallas_call | solution.py:289
  135.2 1.7 fusion.56
  138.0 4.6 multiply_convert_fusion
  142.6 6.3 %fusion.6 = bf16[128,3072]{1,0:T(8,128)(2,1)} fusion(f32[128,3072]{1,0:T(8,128)} %get-tuple-element.163, bf16[128,768]{1,0:T(8,128)(2,1)S(1)} %get-tuple-element.164, bf16[3072,768]{1,0:T(8,128)(2,1)} %all-gather.11.cloned.1.call-done), kind=kOutput, calls=%fused_computation.15 | convolution fusion | flops 614203392 | bytes 7274496 | tf_op jit(solution)/shard_map/dot_general | solution.py:79
  149.0 3.1 multiply_reduce_fusion
  154.4 2.0 fusion.12
  156.5 1.6 convolution_convert_fusion.10
  159.5 1.5 convolution_convert_fusion.8
  166.4 2.4 convolution_convert_fusion
  169.6 2.3 dynamic-slice_bitcast_fusion
  172.8 2.4 collective-permute-start.6
  175.2 4.0 collective-permute-start.7
  180.1 48.5 %attend_back.1 = (bf16[128,1024]{1,0:T(8,128)(2,1)}, bf16[1024,2048]{1,0:T(8,128)(2,1)}, bf16[1024,2048]{1,0:T(8,128)(2,1)}, f32[32,128]{1,0:T(8,128)}, f32[3,128,128]{2,1,0:T(8,128)}) custom-call(s32[4]{0:T(128)} %get-tuple-element.170.lo_ref, s32[4]{0:T(128)} %get-tuple-element.169.hi_ref, bf16[4,16,1024,128]{3,2,1,0:T(8,128)(2,1)} %get-tuple-element.45.p_ref, ...), custom_call_target="tpu_custom_call" | custom-call | flops 60000002048 | bytes 60000000 | tf_op jit(solution)/shard_map/attend_back/pallas_call | solution.py:345
  228.6 7.8 %collective-permute-done.7 = bf16[4,432,384]{2,1,0:T(8,128)(2,1)} collective-permute-done((bf16[4,432,384]{2,1,0:T(8,128)(2,1)}, bf16[4,432,384]{2,1,0:T(8,128)(2,1)}, u32[]{:S(2)}, u32[]{:S(2)}) %collective-permute-start.7) | collective-permute-done | bytes 1327136 | tf_op jit(solution)/shard_map/ppermute | solution.py:905
  236.4 1.6 collective-permute-done.8
  238.0 3.1 fusion.2
  241.1 1.5 copy-done.9
  242.7 32.4 %collective-permute-start.9 = (bf16[432,384]{1,0:T(8,128)(2,1)S(1)}, bf16[432,384]{1,0:T(8,128)(2,1)S(1)}, u32[]{:S(2)}, u32[]{:S(2)}) collective-permute-start(bf16[432,384]{1,0:T(8,128)(2,1)S(1)} %get-tuple-element.58), channel_id=1, source_target_pairs={{0,8},{2,10},{4,12},{6,14},{8,16},{10,18},{12,20},{14,22},{16,24},... | collective-permute-start | bytes 995336 | tf_op jit(solution)/shard_map/ppermute | solution.py:925
  275.1 75.6 %collective-permute-start.10 = (bf16[432,384]{1,0:T(8,128)(2,1)S(1)}, bf16[432,384]{1,0:T(8,128)(2,1)S(1)}, u32[]{:S(2)}, u32[]{:S(2)}) collective-permute-start(bf16[432,384]{1,0:T(8,128)(2,1)S(1)} %get-tuple-element.59), channel_id=1, source_target_pairs={{0,16},{2,18},{4,20},{6,22},{8,24},{10,26},{12,28},{14,30},{16,0},... | collective-permute-start | bytes 995336 | tf_op jit(solution)/shard_map/ppermute | solution.py:925
  352.1 66.5 %finish_rows.1 = (f32[128,768]{1,0:T(8,128)}, f32[144,384]{1,0:T(8,128)}) custom-call(bf16[1024,2048]{1,0:T(8,128)(2,1)} %get-tuple-element.48.dkt_ref, bf16[1024,2048]{1,0:T(8,128)(2,1)} %get-tuple-element.49.dvt_ref, bf16[128,1024]{1,0:T(8,128)(2,1)} %get-tuple-element.56.dq_ref, bf16[2048,768]{1,0:T(8,128)(2,1)} %bitcast.111, bf16[128,768]{1,0:T(8,128)(2,1)} %copy-done.2, ...), custom_call_target="tpu_custom_call" | custom-call | tf_op jit(solution)/shard_map/finish_rows/pallas_call | solution.py:602
  423.7 27.9 %total_over_all.1 = f32[32,8,512]{2,1,0:T(8,128)} custom-call(f32[32,8,512]{2,1,0:T(8,128)} %reshape.274.x_ref), custom_call_target="tpu_custom_call" | custom-call | tf_op jit(solution)/shard_map/total_over_all/pallas_call | solution.py:687
  (235 shorter events, 52.0 us)
Async XLA Ops:
  7.2 10.2 %copy-start = (bf16[128,768]{1,0:T(8,128)(2,1)S(1)}, bf16[128,768]{1,0:T(8,128)(2,1)}, u32[]{:S(2)}) copy-start(bf16[128,768]{1,0:T(8,128)(2,1)} %param.25) | copy-start | bytes 589828
  7.2 60.8 %all-gather.5.cloned.1.call-start = ((), (), s32[]{:S(2)}) async-start(), calls=%async_computation | async-start | bytes 5308416 | tf_op jit(solution)/shard_map/all_gather | solution.py:765
  11.2 124.0 %all-gather.7.cloned.1.call-start = ((), (), s32[]{:S(2)}) async-start(), calls=%async_computation.1 | async-start | bytes 1769472 | tf_op jit(solution)/shard_map/all_gather | solution.py:766
  12.0 126.1 %all-gather.9.cloned.1.call-start = ((), (), s32[]{:S(2)}) async-start(), calls=%async_computation.2 | async-start | bytes 7077888 | tf_op jit(solution)/shard_map/all_gather | solution.py:767
  12.7 129.9 %all-gather.11.cloned.1.call-start = ((), (), s32[]{:S(2)}) async-start(), calls=%async_computation.3 | async-start | bytes 7077888 | tf_op jit(solution)/shard_map/all_gather | solution.py:768
  14.0 147.1 %collective-permute-start.4 = (bf16[128,768]{1,0:T(8,128)(2,1)S(1)}, bf16[128,768]{1,0:T(8,128)(2,1)}, u32[]{:S(2)}, u32[]{:S(2)}) collective-permute-start(bf16[128,768]{1,0:T(8,128)(2,1)S(1)} %get-tuple-element.164), channel_id=1, source_target_pairs={{0,1},{1,0},{2,3},{3,2},{4,5},{5,4},{6,7},{7,6},{8,9},{9,8},{10,11... | collective-permute-start | bytes 589832 | tf_op jit(solution)/shard_map/ppermute | solution.py:30
  14.4 51.4 %copy-start.40 = (bf16[128,32]{0,1:T(8,128)(2,1)S(1)}, bf16[128,32]{0,1:T(8,128)(2,1)}, u32[]{:S(2)}) copy-start(bf16[128,32]{0,1:T(8,128)(2,1)} %param.31) | copy-start | bytes 24580
  19.1 53.1 %copy-start.2 = (bf16[128,768]{1,0:T(8,128)(2,1)}, bf16[128,768]{1,0:T(8,128)(2,1)S(1)}, u32[]{:S(2)}) copy-start(bf16[128,768]{1,0:T(8,128)(2,1)S(1)} %add_convert_fusion.1.x_ref.own_ref) | copy-start | bytes 589828
  62.4 26.7 %copy-start.3 = (bf16[16,128,768]{2,1,0:T(8,128)(2,1)}, bf16[16,128,768]{2,1,0:T(8,128)(2,1)S(1)}, u32[]{:S(2)}) copy-start(bf16[16,128,768]{2,1,0:T(8,128)(2,1)S(1)} %get-tuple-element.42) | copy-start | bytes 9437188
  82.5 6.5 %copy-start.11 = (bf16[768,768]{0,1:T(8,128)(2,1)S(1)}, bf16[768,768]{0,1:T(8,128)(2,1)}, u32[]{:S(2)}) copy-start(bf16[768,768]{0,1:T(8,128)(2,1)} %get-tuple-element.131) | copy-start | bytes 3538948
  134.3 24.8 %collective-permute-start.3 = (bf16[128,384]{1,0:T(8,128)(2,1)}, bf16[128,384]{1,0:T(8,128)(2,1)}, u32[]{:S(2)}, u32[]{:S(2)}) collective-permute-start(bf16[128,384]{1,0:T(8,128)(2,1)} %get-tuple-element.151), channel_id=1, source_target_pairs={{0,1},{1,0},{2,3},{3,2},{4,5},{5,4},{6,7},{7,6},{8,9},{9,8},{10,11... | collective-permute-start | bytes 294920 | tf_op jit(solution)/shard_map/ppermute | solution.py:30
  142.6 11.0 %copy-start.15 = (bf16[128,3072]{1,0:T(8,128)(2,1)}, bf16[128,3072]{1,0:T(8,128)(2,1)S(1)}, u32[]{:S(2)}) copy-start(bf16[128,3072]{1,0:T(8,128)(2,1)S(1)} %get-tuple-element.162) | copy-start | bytes 2359300
  149.0 17.4 %collective-permute-start = (bf16[128,3072]{1,0:T(8,128)(2,1)}, bf16[128,3072]{1,0:T(8,128)(2,1)}, u32[]{:S(2)}, u32[]{:S(2)}) collective-permute-start(bf16[128,3072]{1,0:T(8,128)(2,1)} %fusion.6), channel_id=1, source_target_pairs={{0,1},{1,0},{2,3},{3,2},{4,5},{5,4},{6,7},{7,6},{8,9},{9,8},{10,11... | collective-permute-start | bytes 2359304 | tf_op jit(solution)/shard_map/ppermute | solution.py:30
  153.1 6.4 %collective-permute-start.2 = (bf16[128,768]{1,0:T(8,128)(2,1)}, bf16[128,768]{1,0:T(8,128)(2,1)}, u32[]{:S(2)}, u32[]{:S(2)}) collective-permute-start(bf16[128,768]{1,0:T(8,128)(2,1)} %get-tuple-element.126), channel_id=1, source_target_pairs={{0,1},{1,0},{2,3},{3,2},{4,5},{5,4},{6,7},{7,6},{8,9},{9,8},{10,11... | collective-permute-start | bytes 589832 | tf_op jit(solution)/shard_map/ppermute | solution.py:30
  154.4 6.6 %collective-permute-start.5 = (bf16[128,1536]{1,0:T(8,128)(2,1)}, bf16[128,1536]{1,0:T(8,128)(2,1)S(1)}, u32[]{:S(2)}, u32[]{:S(2)}) collective-permute-start(bf16[128,1536]{1,0:T(8,128)(2,1)} %get-tuple-element.137), channel_id=1, source_target_pairs={{0,1},{1,0},{2,3},{3,2},{4,5},{5,4},{6,7},{7,6},{8,9},{9,8},{10,11... | collective-permute-start | bytes 1179656 | tf_op jit(solution)/shard_map/ppermute | solution.py:30
  156.5 195.0 %copy-start.16 = (bf16[128,768]{1,0:T(8,128)(2,1)}, bf16[128,768]{1,0:T(8,128)(2,1)S(1)}, u32[]{:S(2)}) copy-start(bf16[128,768]{1,0:T(8,128)(2,1)S(1)} %fusion.12) | copy-start | bytes 589828
  159.1 7.3 %collective-permute-start.1 = (bf16[128,384]{1,0:T(8,128)(2,1)S(1)}, bf16[128,384]{1,0:T(8,128)(2,1)S(1)}, u32[]{:S(2)}, u32[]{:S(2)}) collective-permute-start(bf16[128,384]{1,0:T(8,128)(2,1)S(1)} %copy-done.29), channel_id=1, source_target_pairs={{0,1},{1,0},{2,3},{3,2},{4,5},{5,4},{6,7},{7,6},{8,9},{9,8},{10,11... | collective-permute-start | bytes 294920 | tf_op jit(solution)/shard_map/ppermute | solution.py:30
  172.8 55.8 %collective-permute-start.6 = (bf16[4,432,384]{2,1,0:T(8,128)(2,1)}, bf16[4,432,384]{2,1,0:T(8,128)(2,1)}, u32[]{:S(2)}, u32[]{:S(2)}) collective-permute-start(bf16[4,432,384]{2,1,0:T(8,128)(2,1)} %get-tuple-element.130), channel_id=1, source_target_pairs={{0,2},{2,0},{4,6},{6,4},{8,10},{10,8},{12,14},{14,12},{16,18},{18,... | collective-permute-start | bytes 3981320 | tf_op jit(solution)/shard_map/ppermute | solution.py:905
  175.2 61.1 %collective-permute-start.7 = (bf16[4,432,384]{2,1,0:T(8,128)(2,1)}, bf16[4,432,384]{2,1,0:T(8,128)(2,1)}, u32[]{:S(2)}, u32[]{:S(2)}) collective-permute-start(bf16[4,432,384]{2,1,0:T(8,128)(2,1)} %get-tuple-element.129), channel_id=1, source_target_pairs={{0,4},{2,6},{4,0},{6,2},{8,12},{10,14},{12,8},{14,10},{16,20},{18,... | collective-permute-start | bytes 3981320 | tf_op jit(solution)/shard_map/ppermute | solution.py:905
  179.2 58.8 %collective-permute-start.8 = (bf16[4,432,384]{2,1,0:T(8,128)(2,1)S(1)}, bf16[4,432,384]{2,1,0:T(8,128)(2,1)}, u32[]{:S(2)}, u32[]{:S(2)}) collective-permute-start(bf16[4,432,384]{2,1,0:T(8,128)(2,1)S(1)} %get-tuple-element.128), channel_id=1, source_target_pairs={{0,6},{2,4},{4,2},{6,0},{8,14},{10,12},{12,10},{14,8},{16,22},{18,... | collective-permute-start | bytes 3981320 | tf_op jit(solution)/shard_map/ppermute | solution.py:905
  242.6 108.1 %copy-start.34 = (bf16[3,768]{1,0:T(4,128)(2,1)S(1)}, bf16[3,768]{1,0:T(4,128)(2,1)}, u32[]{:S(2)}) copy-start(bf16[3,768]{1,0:T(4,128)(2,1)} %param.37) | copy-start | bytes 13828
  242.6 108.9 %copy-start.37 = (f32[3,1,128]{2,1,0:T(1,128)S(1)}, f32[3,1,128]{2,1,0:T(1,128)}, u32[]{:S(2)}) copy-start(f32[3,1,128]{2,1,0:T(1,128)} %param.39) | copy-start | bytes 4612
  242.6 109.1 %copy-start.35 = (f32[32,128]{1,0:T(8,128)S(1)}, f32[32,128]{1,0:T(8,128)}, u32[]{:S(2)}) copy-start(f32[32,128]{1,0:T(8,128)} %get-tuple-element.63) | copy-start | bytes 49156
  242.6 109.3 %copy-start.24 = (f32[3,128,128]{2,1,0:T(8,128)S(1)}, f32[3,128,128]{2,1,0:T(8,128)}, u32[]{:S(2)}) copy-start(f32[3,128,128]{2,1,0:T(8,128)} %get-tuple-element.62) | copy-start | bytes 589828
  242.7 175.8 %collective-permute-start.9 = (bf16[432,384]{1,0:T(8,128)(2,1)S(1)}, bf16[432,384]{1,0:T(8,128)(2,1)S(1)}, u32[]{:S(2)}, u32[]{:S(2)}) collective-permute-start(bf16[432,384]{1,0:T(8,128)(2,1)S(1)} %get-tuple-element.58), channel_id=1, source_target_pairs={{0,8},{2,10},{4,12},{6,14},{8,16},{10,18},{12,20},{14,22},{16,24},... | collective-permute-start | bytes 995336 | tf_op jit(solution)/shard_map/ppermute | solution.py:925
  275.1 143.5 %collective-permute-start.10 = (bf16[432,384]{1,0:T(8,128)(2,1)S(1)}, bf16[432,384]{1,0:T(8,128)(2,1)S(1)}, u32[]{:S(2)}, u32[]{:S(2)}) collective-permute-start(bf16[432,384]{1,0:T(8,128)(2,1)S(1)} %get-tuple-element.59), channel_id=1, source_target_pairs={{0,16},{2,18},{4,20},{6,22},{8,24},{10,26},{12,28},{14,30},{16,0},... | collective-permute-start | bytes 995336 | tf_op jit(solution)/shard_map/ppermute | solution.py:925
  350.7 67.9 %collective-permute-start.11 = (bf16[432,384]{1,0:T(8,128)(2,1)S(1)}, bf16[432,384]{1,0:T(8,128)(2,1)S(1)}, u32[]{:S(2)}, u32[]{:S(2)}) collective-permute-start(bf16[432,384]{1,0:T(8,128)(2,1)S(1)} %get-tuple-element.60), channel_id=1, source_target_pairs={{0,24},{2,26},{4,28},{6,30},{8,0},{10,2},{12,4},{14,6},{16,8},{18,... | collective-permute-start | bytes 995336 | tf_op jit(solution)/shard_map/ppermute | solution.py:925
  352.0 66.6 %copy-start.32 = (f32[768]{0:T(1024)S(1)}, f32[768]{0:T(1024)}, u32[]{:S(2)}) copy-start(f32[768]{0:T(1024)} %param.26) | copy-start | bytes 9220
  352.0 66.6 %copy-start.39 = (f32[128]{0:T(128)S(1)}, f32[128]{0:T(128)}, u32[]{:S(2)}) copy-start(f32[128]{0:T(128)} %copy-done.38) | copy-start | bytes 1540
  352.0 66.6 %copy-start.42 = (f32[128]{0:T(128)S(1)}, f32[128]{0:T(128)}, u32[]{:S(2)}) copy-start(f32[128]{0:T(128)} %copy-done.41) | copy-start | bytes 1540
  352.1 68.0 %copy-start.18 = (f32[128,768]{1,0:T(8,128)S(1)}, f32[128,768]{1,0:T(8,128)}, u32[]{:S(2)}) copy-start(f32[128,768]{1,0:T(8,128)} %get-tuple-element.127) | copy-start | bytes 1179652
  455.8 7.2 %copy-start.1 = (bf16[128,768]{1,0:T(8,128)(2,1)S(1)}, bf16[128,768]{1,0:T(8,128)(2,1)}, u32[]{:S(2)}) copy-start(bf16[128,768]{1,0:T(8,128)(2,1)} %param.25) | copy-start | bytes 589828
  (36 other events, 107.4 us)
Sparse Core Ops, SparseCore 0:
  11.3 15.2 all-gather.4
  28.2 10.3 all-gather.6
  40.2 15.5 all-gather.8
  57.2 15.6 all-gather.10

commit v3 on v2

--- a/solution.py
+++ b/solution.py
@@ -190,6 +190,7 @@
     groups = q_ref.shape[1] // GW
     rows = QB * HG
     scale = head_dim ** (-0.5)
+    used = head_dim * HG
     mask = head_mask(head_dim)
 
     @pl.when(block == 0)
@@ -203,11 +204,11 @@
         lanes = slice(g * GW, (g + 1) * GW)
         here = slice(g * rows, (g + 1) * rows)
         inverse = rl_ref[here, 0:1]
-        qext[g] = jnp.transpose(expand(q_ref[:, lanes].astype(f32), mask)).astype(bf16)
+        qext[g] = jnp.transpose(expand(q_ref[:, lanes].astype(f32), mask))[:used, :].astype(bf16)
         grads = do_ref[:, lanes].astype(f32)
         both = expand(grads, mask) * inverse
         doexp[g] = both.astype(bf16)
-        doext[g] = jnp.transpose(both).astype(bf16)
+        doext[g] = jnp.transpose(both)[:used, :].astype(bf16)
         mixed = jnp.sum(expand(grads * o_ref[:, lanes], mask), axis=1, keepdims=True) * inverse
         delta[here, :] = jnp.broadcast_to(mixed, (rows, TILE))
         dqacc[g] = jnp.zeros((rows, GW), f32)
@@ -220,14 +221,15 @@
             for g in (2 * pair, 2 * pair + 1):
                 lanes = slice(g * GW, (g + 1) * GW)
                 here = slice(g * rows, (g + 1) * rows)
+                feats = slice(g * used, (g + 1) * used)
                 low = p_ref[0, tile, here, :]
                 dp = jnp.dot(doexp[g], vt_ref[tile, lanes, :], preferred_element_type=f32)
                 gl = low.astype(f32) * (dp - delta[here, :])
                 grads.append(gl)
                 gl_low = gl.astype(bf16)
                 dqacc[g] += jnp.dot(gl_low, k_ref[tile, :, lanes], preferred_element_type=f32)
-                dkt_acc[lanes, keys] += jnp.dot(qext[g], gl_low, preferred_element_type=f32)
-                dvt_acc[lanes, keys] += jnp.dot(doext[g], low, preferred_element_type=f32)
+                dkt_acc[feats, keys] += jnp.dot(qext[g], gl_low, preferred_element_type=f32)
+                dvt_acc[feats, keys] += jnp.dot(doext[g], low, preferred_element_type=f32)
             for i in range(QB):
                 at = slice(i * HG, (i + 1) * HG)
                 glow[pair * 16 : (pair + 1) * 16, i * TILE : (i + 1) * TILE] = jnp.concatenate(
@@ -341,6 +343,7 @@
     rows = QB * HG
     blocks = q.shape[0] // QB
     kernels, heads = wp.shape
+    used = HG * head_dim
     by_block = lambda b, *_: (b, 0)
     return pl.pallas_call(
         functools.partial(bwd_kernel, head_dim),
@@ -364,29 +367,29 @@
             ],
             out_specs=[
                 pl.BlockSpec((QB, wide), by_block),
-                whole((wide, tiles * TILE)),
-                whole((wide, tiles * TILE)),
+                whole((groups * used, tiles * TILE)),
+                whole((groups * used, tiles * TILE)),
                 whole((heads, kernels)),
                 whole((3, kernels, TILE)),
             ],
             scratch_shapes=[
-                pltpu.VMEM((groups, GW, rows), bf16),
+                pltpu.VMEM((groups, used, rows), bf16),
                 pltpu.VMEM((groups, rows, GW), bf16),
-                pltpu.VMEM((groups, GW, rows), bf16),
+                pltpu.VMEM((groups, used, rows), bf16),
                 pltpu.VMEM((groups * rows, TILE), f32),
                 pltpu.VMEM((groups, rows, GW), f32),
                 pltpu.VMEM((heads, QB * TILE), bf16),
                 pltpu.VMEM((QB, TILE), f32),
                 pltpu.VMEM((kernels, QB * TILE), bf16),
                 pltpu.VMEM((kernels, QB * TILE), f32),
-                pltpu.VMEM((wide, tiles * TILE), f32),
-                pltpu.VMEM((wide, tiles * TILE), f32),
+                pltpu.VMEM((groups * used, tiles * TILE), f32),
+                pltpu.VMEM((groups * used, tiles * TILE), f32),
             ],
         ),
         out_shape=[
             jax.ShapeDtypeStruct(q.shape, bf16),
-            jax.ShapeDtypeStruct((wide, tiles * TILE), bf16),
-            jax.ShapeDtypeStruct((wide, tiles * TILE), bf16),
+            jax.ShapeDtypeStruct((groups * used, tiles * TILE), bf16),
+            jax.ShapeDtypeStruct((groups * used, tiles * TILE), bf16),
             jax.ShapeDtypeStruct((heads, kernels), f32),
             jax.ShapeDtypeStruct((3, kernels, TILE), f32),
         ],
@@ -427,73 +430,231 @@
     )
 
 
-def gather_kernel(outers, x_ref, c_ref, xo_ref, co_ref, sends, gets, sends_c, gets_c):
+def front_kernel(
+    atoms_ref, og_ref, sm_ref, c_ref, w_ref, code_ref, table_ref, gain_ref, shift_ref,
+    base_ref, ogo_ref, smo_ref, every_ref, co_ref, wo_ref, wq_ref, q_ref, k_ref, kt_ref, v_ref, vt_ref,
+    dealt, own, wpad, k_st, kt_st, v_st, vt_st,
+    deal_s, deal_r, w_sems, sends, gets, sends_c, gets_c, outs,
+):
     row, core, outer, inner = places()
+    outers, shards = every_ref.shape[0], every_ref.shape[1]
+    width = own.shape[2]
+    groups = q_ref.shape[1] // GW
+    used = width // groups
     mates = plane_mates(inner)
     far = [(outer + step) % outers for step in range(1, outers)]
     plane = [(outer * INNER + mate, core) for mate in mates]
     column = [(other * INNER + inner, core) for other in far]
-    greet(plane + column)
+    barrier = pltpu.get_barrier_semaphore()
+    for target in plane + column + [(row, 1 - core)]:
+        pl.semaphore_signal(barrier, inc=1, device_id=target, device_id_type=MESH)
+    for m in range(outers):
+        @pl.when(m * INNER + outer != row)
+        def _():
+            pl.semaphore_signal(
+                barrier, inc=1, device_id=(m * INNER + outer, core), device_id_type=MESH
+            )
+    pl.semaphore_wait(barrier, outers + 2 * INNER - 1 - jnp.where(outer == inner, 1, 0))
+
+    dealing = ((atoms_ref, dealt), (sm_ref, smo_ref), (og_ref, ogo_ref))
+
+    def deal(q, slot, target, which=(0, 1, 2)):
+        return [
+            remote(
+                dealing[at][0].at[q], dealing[at][1].at[slot], deal_s.at[q, at], deal_r.at[slot, at],
+                (target, core),
+            )
+            for at in which
+        ]
+
+    for q in range(INNER):
+        target = inner * INNER + q
+
+        @pl.when(target != row)
+        def _():
+            for copy in deal(q, outer, target):
+                copy.start()
+
+        @pl.when(target == row)
+        def _():
+            dealt[outer] = atoms_ref[q]
+            smo_ref[outer] = sm_ref[q]
+            ogo_ref[outer] = og_ref[q]
+
+    to_core = remote(w_ref, wo_ref.at[core], w_sems.at[0], w_sems.at[1], (row, 1 - core))
+    to_core.start()
+    wo_ref[core] = w_ref[...]
+    co_ref[row] = c_ref[...]
+    wpad[...] = jnp.zeros(wpad.shape, bf16)
+
+    for m in range(outers):
+        @pl.when(m * INNER + outer != row)
+        def _():
+            for copy in deal(0, m, m * INNER + outer, (0, 1)):
+                copy.wait_recv()
+
+    small = smo_ref[0]
+    for m in range(1, outers):
+        small = small + smo_ref[m]
+    kinds = lax.broadcasted_iota(jnp.int32, (table_ref.shape[0], own.shape[0] * own.shape[1]), 0)
+    hot = jnp.where(kinds.astype(f32) == small[0:1, :], 1.0, 0.0).astype(bf16)
+    base = (
+        dealt[...].astype(f32).reshape(base_ref.shape)
+        + code_ref[...]
+        + lax.dot_general(hot, table_ref[...], (((0,), (0,)), ((), ())), preferred_element_type=f32)
+    )
+    base_ref[...] = base
+    normed, _ = norm_parts(base)
+    normed_in = (normed * gain_ref[...] + shift_ref[...]).astype(bf16)
+    own[...] = normed_in.reshape(own.shape)
+    every_ref[:, row] = own[...]
     started = []
 
     def send(src, src_c, slot, target):
         at = len(started) // 2
         for copy in (
-            remote(src, xo_ref.at[slot], sends.at[at], gets.at[slot], target),
+            remote(src, every_ref.at[:, slot], sends.at[at], gets.at[slot], target),
             remote(src_c, co_ref.at[slot], sends_c.at[at], gets_c.at[slot], target),
         ):
             copy.start()
             started.append(copy)
 
-    for target in column:
-        send(x_ref, c_ref, row, target)
-    for target in plane:
-        send(x_ref, c_ref, row, target)
-    xo_ref[row] = x_ref[...]
-    co_ref[row] = c_ref[...]
+    for target in column + plane:
+        send(own, c_ref, row, target)
+
+    to_core.wait_recv()
+    for half in range(2):
+        here = slice(half * w_ref.shape[0], (half + 1) * w_ref.shape[0])
+        for part in range(3):
+            for g in range(groups):
+                lane = part * width + g * used
+                first, last = lane // 128 * 128, -(-(lane + used) // 128) * 128
+                piece = wo_ref[half, :, first:last]
+                wpad[here, part * groups * GW + g * GW : part * groups * GW + g * GW + used] = piece[
+                    :, lane - first : lane - first + used
+                ]
 
     def arrived(slot):
-        remote(x_ref, xo_ref.at[slot], sends.at[0], gets.at[slot], (row, core)).wait_recv()
+        remote(own, every_ref.at[:, slot], sends.at[0], gets.at[slot], (row, core)).wait_recv()
         remote(c_ref, co_ref.at[slot], sends_c.at[0], gets_c.at[slot], (row, core)).wait_recv()
 
     for step in range(1, outers):
         slot = ((outer + outers - step) % outers) * INNER + inner
         arrived(slot)
         for target in plane:
-            send(xo_ref.at[slot], co_ref.at[slot], slot, target)
-    for mate in mates:
-        for step in range(outers):
-            arrived(((outer + outers - step) % outers) * INNER + mate)
+            send(every_ref.at[:, slot], co_ref.at[slot], slot, target)
+
+    wide = groups * GW
+    wq_ref[...] = wpad[:, :wide]
+    q_ref[...] = jnp.dot(
+        own[...].reshape(base_ref.shape), wpad[:, :wide], preferred_element_type=f32
+    ).astype(bf16)
+
+    def store(slot, tile):
+        return [
+            pltpu.make_async_copy(src.at[slot], dst.at[tile], outs.at[slot, at])
+            for at, (src, dst) in enumerate(((k_st, k_ref), (kt_st, kt_ref), (v_st, v_ref), (vt_st, vt_ref)))
+        ]
+
+    def project(step, carry):
+        a = (outer + outers - step // outers) % outers
+        m = step % outers
+        tile = m * INNER + a
+        slot = step % 2
+
+        @pl.when(m == 0)
+        def _():
+            for mate in mates:
+                arrived(a * INNER + mate)
+
+        @pl.when(step >= 2)
+        def _():
+            for copy in store(slot, tile):
+                copy.wait()
+
+        x = every_ref[m, pl.ds(a * INNER, INNER)].reshape(base_ref.shape)
+        key = jnp.dot(x, wpad[:, wide : 2 * wide], preferred_element_type=f32)
+        k_st[slot] = key.astype(bf16)
+        kt_st[slot] = jnp.transpose(key).astype(bf16)
+        value = jnp.dot(x, wpad[:, 2 * wide :], preferred_element_type=f32)
+        v_st[slot] = value.astype(bf16)
+        vt_st[slot] = jnp.transpose(value).astype(bf16)
+        for copy in store(slot, tile):
+            copy.start()
+        return carry
+
+    lax.fori_loop(0, shards, project, 0)
+    for slot in range(2):
+        for copy in store(slot, slot):
+            copy.wait()
+    for m in range(outers):
+        @pl.when(m * INNER + outer != row)
+        def _():
+            for copy in deal(0, m, m * INNER + outer, (2,)):
+                copy.wait_recv()
+    for q in range(INNER):
+        @pl.when(inner * INNER + q != row)
+        def _():
+            for copy in deal(q, outer, inner * INNER + q):
+                copy.wait_send()
+    to_core.wait_send()
     for copy in started:
         copy.wait_send()
 
 
-def gather_rows(x, c, rows):
+def front(atoms, og, sm, c, w_half, code, table, gain, shift, rows, heads):
     outers = rows // INNER
     count = (outers - 1) + 3 * outers
+    quarter, width = atoms.shape[1:]
+    total = INNER * quarter
+    wide = heads // HG * GW
+    tiles = rows * total // TILE
     vmem = pl.BlockSpec(memory_space=pltpu.VMEM)
+    hbm = pl.BlockSpec(memory_space=pl.ANY)
+    shape = jax.ShapeDtypeStruct
     return pl.pallas_call(
-        functools.partial(gather_kernel, outers),
+        front_kernel,
         out_shape=[
-            jax.ShapeDtypeStruct((rows,) + x.shape, x.dtype),
-            jax.ShapeDtypeStruct((rows,) + c.shape, c.dtype),
+            shape((total, width), f32),
+            shape(og.shape, bf16),
+            shape(sm.shape, f32),
+            shape((outers, rows, quarter, width), bf16),
+            shape((rows,) + c.shape, bf16),
+            shape((2,) + w_half.shape, bf16),
+            shape((width, wide), bf16),
+            shape((total, wide), bf16),
+            shape((tiles, TILE, wide), bf16),
+            shape((tiles, wide, TILE), bf16),
+            shape((tiles, TILE, wide), bf16),
+            shape((tiles, wide, TILE), bf16),
         ],
-        in_specs=[vmem, vmem],
-        out_specs=[vmem, vmem],
+        in_specs=[vmem] * 9,
+        out_specs=[vmem] * 8 + [hbm] * 4,
         scratch_shapes=[
+            pltpu.VMEM((outers, quarter, width), bf16),
+            pltpu.VMEM((outers, quarter, width), bf16),
+            pltpu.VMEM((width, 3 * wide), bf16),
+            pltpu.VMEM((2, TILE, wide), bf16),
+            pltpu.VMEM((2, wide, TILE), bf16),
+            pltpu.VMEM((2, TILE, wide), bf16),
+            pltpu.VMEM((2, wide, TILE), bf16),
+            pltpu.SemaphoreType.DMA((INNER, 3)),
+            pltpu.SemaphoreType.DMA((outers, 3)),
+            pltpu.SemaphoreType.DMA((2,)),
             pltpu.SemaphoreType.DMA((count,)),
             pltpu.SemaphoreType.DMA((rows,)),
             pltpu.SemaphoreType.DMA((count,)),
             pltpu.SemaphoreType.DMA((rows,)),
+            pltpu.SemaphoreType.DMA((2, 4)),
         ],
         compiler_params=pltpu.CompilerParams(
-            collective_id=0, has_side_effects=True, vmem_limit_bytes=40 << 20
+            collective_id=0, has_side_effects=True, vmem_limit_bytes=60 << 20
         ),
-        name="gather_rows",
-    )(x, c)
-
-
-def finish_kernel(outers, part_width, dkt_ref, dvt_ref, dq_ref, every_ref, own_ref, wq_ref, wk_ref, wv_ref, xo_ref, wo_ref,
+        name="front",
+    )(atoms, og, sm, c, w_half, code, table, gain, shift)
+
+
+def finish_kernel(outers, part_width, dkt_ref, dvt_ref, dq_ref, every_ref, own_ref, wq_ref, w_ref, xo_ref, wo_ref,
                   xs, xa, xm, xb, wp, wi, wa, wm, wb, w0_sems, a_send, a_recv, b_send, b_recv):
     row, core, outer, inner = places()
     mates = plane_mates(inner)
@@ -508,11 +669,24 @@
     greet(plane + column + [(row, 1 - core)])
     started = []
 
-    def grad_chunk(slot):
-        at = pl.ds(pl.multiple_of(slot * count, count), count)
-        flipped = jnp.dot(wk_ref[...], dkt_ref[:, at], preferred_element_type=f32)
-        flipped += jnp.dot(wv_ref[...], dvt_ref[:, at], preferred_element_type=f32)
-        return jnp.transpose(flipped)
+    quarter = count // INNER
+
+    def grad_tile(tile):
+        at = pl.ds(pl.multiple_of(tile * TILE, TILE), TILE)
+        flipped = jnp.dot(w_ref[:, width : 2 * width], dkt_ref[:, at], preferred_element_type=f32)
+        flipped += jnp.dot(w_ref[:, 2 * width :], dvt_ref[:, at], preferred_element_type=f32)
+        return jnp.transpose(flipped).astype(bf16)
+
+    def grad_plane(o):
+        def one(m, carry):
+            block = grad_tile(m * INNER + o)
+            for i in range(INNER):
+                xs[o, i, pl.ds(pl.multiple_of(m * quarter, quarter), quarter), :] = block[
+                    i * quarter : (i + 1) * quarter, :
+                ]
+            return carry
+
+        lax.fori_loop(0, outers, one, 0)
 
     def begin(copy):
         copy.start()
@@ -522,15 +696,12 @@
         return remote(src, dst, a_send.at[which, p, at], a_recv.at[which, p, o], plane[p])
 
     for at, o in enumerate(order):
+        grad_plane(o)
         for p in range(3):
-            xs[o, mates[p]] = grad_chunk(o * INNER + mates[p]).astype(bf16)
             begin(to_mate(0, at, o, p, xs.at[o, mates[p]], xa.at[p, o]))
-    for o in order:
-        xs[o, inner] = grad_chunk(o * INNER + inner).astype(bf16)
-
     def key_part(index, carry):
         g = index
-        here = pl.ds(pl.multiple_of(g * GW, GW), used)
+        here = pl.ds(pl.multiple_of(g * used, 16), used)
         there = pl.ds(pl.multiple_of(g * used, 16), used)
         wp[there, :] = lax.dot_general(
             dq_ref[:, pl.ds(pl.multiple_of(g * GW, GW), GW)], own_ref[...], (((0,), (0,)), ((), ())),
@@ -593,7 +764,7 @@
         copy.wait_send()
 
 
-def finish_rows(dkt, dvt, dq, every, own, w_q, w_k, w_v, rows, head_dim):
+def finish_rows(dkt, dvt, dq, every, own, w_q, w, rows, head_dim):
     outers = rows // INNER
     count, width = own.shape
     each = 3 * width // rows
@@ -605,7 +776,7 @@
             jax.ShapeDtypeStruct((count, width), f32),
             jax.ShapeDtypeStruct((each, half), f32),
         ],
-        in_specs=[vmem] * 8,
+        in_specs=[vmem] * 7,
         out_specs=[vmem] * 2,
         scratch_shapes=[
             pltpu.VMEM((outers, INNER, count, width), bf16),
@@ -627,11 +798,14 @@
             collective_id=1, has_side_effects=True, vmem_limit_bytes=60 << 20
         ),
         name="finish_rows",
-    )(dkt, dvt, dq, every, own, w_q, w_k, w_v)
-
-
-def total_kernel(count, x_ref, out_ref, got, s1, r1, s2, r2):
-    row, core = lax.axis_index("row"), lax.axis_index("wt")
+    )(dkt, dvt, dq, every, own, w_q, w)
+
+
+def total_kernel(
+    count, x_ref, ag_ref, bo_ref, fo_ref, out_ref, ago_ref, boo_ref, foo_ref,
+    got, s1, r1, s2, r2, back_s, back_r,
+):
+    row, core, outer, inner = places()
     me = row * 2 + core
     barrier = pltpu.get_barrier_semaphore()
 
@@ -675,24 +849,63 @@
         second(step).wait_send()
         return carry
 
+    def back(m, slot, target):
+        return [
+            remote(src, dst.at[slot], back_s.at[m, at], back_r.at[slot, at], (target, core))
+            for at, (src, dst) in enumerate(
+                ((ag_ref.at[m], ago_ref), (bo_ref.at[m], boo_ref), (fo_ref, foo_ref))
+            )
+        ]
+
     lax.fori_loop(1, count, start_first, 0)
+    for m in range(ag_ref.shape[0]):
+        owner = m * INNER + outer
+
+        @pl.when(owner != row)
+        def _():
+            for copy in back(m, inner, owner):
+                copy.start()
+
+        @pl.when(owner == row)
+        def _():
+            ago_ref[inner] = ag_ref[m]
+            boo_ref[inner] = bo_ref[m]
+            foo_ref[inner] = fo_ref[...]
+
     out_ref[me] = lax.fori_loop(1, count, add, x_ref[me])
     lax.fori_loop(1, count, start_second, 0)
+    for q in range(INNER):
+        @pl.when(inner * INNER + q != row)
+        def _():
+            for copy in back(0, q, inner * INNER + q):
+                copy.wait_recv()
+    for m in range(ag_ref.shape[0]):
+        @pl.when(m * INNER + outer != row)
+        def _():
+            for copy in back(m, inner, m * INNER + outer):
+                copy.wait_send()
     lax.fori_loop(1, count, end, 0)
 
 
-def total_over_all(x):
+def total_over_all(x, ag, bo, fo):
     count = x.shape[0]
     vmem = pl.BlockSpec(memory_space=pltpu.VMEM)
+    shape = jax.ShapeDtypeStruct
     return pl.pallas_call(
         functools.partial(total_kernel, count),
-        out_shape=jax.ShapeDtypeStruct(x.shape, f32),
-        in_specs=[vmem],
-        out_specs=vmem,
-        scratch_shapes=[pltpu.VMEM(x.shape, f32)] + [pltpu.SemaphoreType.DMA((count,))] * 4,
-        compiler_params=pltpu.CompilerParams(collective_id=2, has_side_effects=True),
+        out_shape=[
+            shape(x.shape, f32), shape(ag.shape, f32), shape(bo.shape, bf16), shape((INNER,) + fo.shape, f32)
+        ],
+        in_specs=[vmem] * 4,
+        out_specs=[vmem] * 4,
+        scratch_shapes=[pltpu.VMEM(x.shape, f32)]
+        + [pltpu.SemaphoreType.DMA((count,))] * 4
+        + [pltpu.SemaphoreType.DMA((INNER, 3))] * 2,
+        compiler_params=pltpu.CompilerParams(
+            collective_id=2, has_side_effects=True, vmem_limit_bytes=40 << 20
+        ),
         name="total_over_all",
-    )(x)
+    )(x, ag, bo, fo)
 
 
 def on_device(
@@ -728,6 +941,7 @@
     all_rows = row_count * row_size
     groups = head_count // HG
     used = HG * head_dim
+    dealt = row_size == INNER * INNER and row_count == INNER * QB
     covers = row_size <= 2 * reach_shards + 1
     span = row_size if covers else 2 * reach_shards + 1
     key_count = span * row_count
@@ -762,16 +976,15 @@
         split = lax.slice_in_dim(split, 0, used, axis=axis + 1)
         return split.reshape(x.shape[:axis] + (groups * used,) + x.shape[axis + 1 :])
 
-    w_qkv_full = lax.all_gather(w_qkv, "wt", axis=0, tiled=True)
     w_out_full = lax.all_gather(w_out, "wt", axis=0, tiled=True)
     w_up_full = lax.all_gather(w_up, "wt", axis=0, tiled=True)
     w_down_full = lax.all_gather(w_down, "wt", axis=0, tiled=True)
-    w_q = padded(w_qkv_full[:, :model_width], 1)
-    w_k = padded(w_qkv_full[:, model_width : 2 * model_width], 1)
-    w_v = padded(w_qkv_full[:, 2 * model_width :], 1)
-
     item_ends = jnp.cumsum(lengths[0])
-    own_places = my_index * row_count + jnp.arange(row_count, dtype=jnp.int32)
+    if dealt:
+        chunk = jnp.arange(row_count, dtype=jnp.int32)
+        own_places = chunk // QB * (row_size * QB) + my_index * QB + chunk % QB
+    else:
+        own_places = my_index * row_count + jnp.arange(row_count, dtype=jnp.int32)
     own_ids = item_ids(own_places, item_ends)
     key_places = key_base + jnp.arange(key_count, dtype=jnp.int32)
     inside = (key_places >= 0) & (key_places < all_rows)
@@ -786,33 +999,59 @@
     lo = jnp.clip((begins - key_base) // TILE, 0, tiles)
     hi = jnp.clip((ends - key_base + TILE - 1) // TILE, 0, tiles)
 
-    onehot = (atom_types[0][:, None] == type_codes[None, :]).astype(bf16)
-    base_rows = (
-        atoms[0].astype(f32)
-        + time_code(times[0], model_width)
-        + jnp.dot(onehot, type_table, preferred_element_type=f32)
-    )
-    normed_one, inverse_one = norm_parts(base_rows)
-    normed_in = (normed_one * gain_one + shift_one).astype(bf16)
-    if covers:
+    wide = groups * GW
+    code = time_code(times[0], model_width)
+    outer, inner = my_index // INNER, my_index % INNER
+    outers = row_size // INNER
+    if dealt:
+        quarters = lambda x: x.reshape((INNER, QB) + x.shape[1:])
+        notes = jnp.concatenate(
+            [atom_types[0].astype(f32)[None], force_grad[:, 0, :], jnp.zeros((4, row_count), f32)], axis=0
+        )
+        notes = jnp.swapaxes(notes.reshape(8, INNER, QB), 0, 1)
+        lane_chunk = jnp.arange(row_count, dtype=jnp.int32) // QB
+        notes = jnp.where(lane_chunk == outer, jnp.tile(notes, (1, 1, INNER)), 0.0)
         low_pos = jnp.pad(coords[:, 0, :], ((0, 13), (0, 0)))
-        every, every_pos = gather_rows(normed_in, low_pos, row_size)
+        (
+            base_rows, og_rows, notes, every, every_pos, w_qkv_full, w_q, queries, keys, keys_t, values, values_t
+        ) = front(
+            quarters(atoms[0]), quarters(out_grad[0]), notes, low_pos, w_qkv, code[None], type_table,
+            gain_one[None], shift_one[None], row_size, head_count,
+        )
+        og_rows = og_rows.reshape(row_count, model_width)
+        notes = jnp.sum(notes, axis=0)
+        kinds, force_cot = notes[0].astype(jnp.int32), notes[1:4]
         every = every.reshape(key_count, model_width)
+        w_qkv_full = w_qkv_full.reshape(model_width, 3 * model_width)
         kpos = every_pos[:, :3, :].astype(f32)
+        own_pos = jnp.swapaxes(kpos, 0, 1).reshape(3, outers, row_size, QB)
+        own_pos = lax.dynamic_index_in_dim(own_pos, my_index, 2, False).reshape(3, row_count)
+        onehot = (kinds[:, None] == type_codes[None, :]).astype(bf16)
+        normed_one, inverse_one = norm_parts(base_rows)
+        normed_in = (normed_one * gain_one + shift_one).astype(bf16)
     else:
+        w_qkv_full = lax.all_gather(w_qkv, "wt", axis=0, tiled=True)
+        w_q = padded(w_qkv_full[:, :model_width], 1)
+        w_k = padded(w_qkv_full[:, model_width : 2 * model_width], 1)
+        w_v = padded(w_qkv_full[:, 2 * model_width :], 1)
+        og_rows, force_cot, own_pos = out_grad[0], force_grad[:, 0, :], coords[:, 0, :].astype(f32)
+        onehot = (atom_types[0][:, None] == type_codes[None, :]).astype(bf16)
+        base_rows = (
+            atoms[0].astype(f32) + code + jnp.dot(onehot, type_table, preferred_element_type=f32)
+        )
+        normed_one, inverse_one = norm_parts(base_rows)
+        normed_in = (normed_one * gain_one + shift_one).astype(bf16)
         every = fetch(normed_in, 0)
         positions = fetch(coords[:, 0, :], 1).astype(f32)
         kpos = jnp.swapaxes(positions.reshape(3, tiles, TILE), 0, 1)
-
-    queries = jnp.dot(normed_in, w_q, preferred_element_type=f32).astype(bf16)
-    keys = jnp.dot(every, w_k, preferred_element_type=f32).astype(bf16)
-    values = jnp.dot(every, w_v, preferred_element_type=f32).astype(bf16)
-    wide = groups * GW
-    by_tile = lambda x: x.reshape(tiles, TILE, wide)
-    keys, values = by_tile(keys), by_tile(values)
-    keys_t = jnp.swapaxes(keys, 1, 2)
-    values_t = jnp.swapaxes(values, 1, 2)
-    qpos = jnp.transpose(coords[:, 0, :].astype(f32))
+        queries = jnp.dot(normed_in, w_q, preferred_element_type=f32).astype(bf16)
+        keys = jnp.dot(every, w_k, preferred_element_type=f32).astype(bf16)
+        values = jnp.dot(every, w_v, preferred_element_type=f32).astype(bf16)
+        by_tile = lambda x: x.reshape(tiles, TILE, wide)
+        keys, values = by_tile(keys), by_tile(values)
+        keys_t = jnp.swapaxes(keys, 1, 2)
+        values_t = jnp.swapaxes(values, 1, 2)
+    qpos = jnp.transpose(own_pos)
     qid = own_ids[:, None]
     kid = key_ids.reshape(tiles, 1, TILE)
     steep = math.sqrt(0.5 * LOG2E)
@@ -835,8 +1074,7 @@
     block_sum = after_att + jnp.dot(activated, w_down_full, preferred_element_type=f32)
     out_low = block_sum.astype(bf16)
     force_rows = along_rows(w_force, out_low)
-    force_cot = force_grad[:, 0, :]
-    grad_sum = out_grad[0].astype(f32) + lax.dot_general(
+    grad_sum = og_rows.astype(f32) + lax.dot_general(
         force_cot,
         w_force.astype(f32),
         (((0,), (0,)), ((), ())),
@@ -891,9 +1129,6 @@
             jnp.transpose(total[up : up + out]),
             jnp.transpose(jnp.concatenate([x for x in down], axis=1)),
         )
-
-    outer, inner = my_index // INNER, my_index % INNER
-    outers = row_size // INNER
 
     def by_plane(x, which):
         return lax.dynamic_index_in_dim(x.reshape((outers, INNER) + x.shape[1:]), which, 1, False)
@@ -932,7 +1167,7 @@
 
     do_wide = padded(grad_att_low, 1)
     do_wide, ffn_grads = lax.optimization_barrier((do_wide, ffn_grads))
-    if covers:
+    if dealt:
         arrived = to_planes()
     else:
         summed = lax.psum_scatter(ffn_grads, "row", scatter_dimension=0, tiled=False).astype(f32)
@@ -941,24 +1176,29 @@
         lo, hi, probs, inverse_total, queries, do_wide, att_wide, keys, values_t,
         qpos, kpos, cen, amp, lnorm, w_pair, head_dim,
     )
-    if covers:
+    if dealt:
         dq, arrived = lax.optimization_barrier((dq, arrived))
         own_sum, others = plane_sums(arrived)
         dq, others = lax.optimization_barrier((dq, others))
         far_sums = to_columns(others)
         grad_normed_in, w_qkv_grad_t = finish_rows(
-            dkt, dvt, dq, every, normed_in, w_q, w_k, w_v, row_size, head_dim
+            dkt, dvt, dq, every, normed_in, w_q, w_qkv_full, row_size, head_dim
         )
         grad_normed_in, far_sums = lax.optimization_barrier((grad_normed_in, far_sums))
         summed = own_sum + sum(x.astype(f32) for x in far_sums)
         w_qkv_grad = jnp.transpose(w_qkv_grad_t)
     else:
         key_grad, value_grad = jnp.transpose(dkt), jnp.transpose(dvt)
-        grad_every = along_rows(key_grad, w_k) + along_rows(value_grad, w_v)
+        grad_every = along_rows(key_grad, w_qkv_full[:, model_width : 2 * model_width])
+        grad_every += along_rows(value_grad, w_qkv_full[:, 2 * model_width :])
         grad_normed_in = along_rows(dq, w_q) + send_back(grad_every)
-        parts = [(normed_in, dq), (every, key_grad), (every, value_grad)]
         whole_grad = jnp.concatenate(
-            [unpadded(cross_rows(right, left), 0) for left, right in parts], axis=0
+            [
+                unpadded(cross_rows(dq, normed_in), 0),
+                cross_rows(key_grad, every),
+                cross_rows(value_grad, every),
+            ],
+            axis=0,
         ).astype(bf16)
         half_grad = lax.psum_scatter(whole_grad, "wt", scatter_dimension=1, tiled=True)
         w_qkv_grad = over_rows(half_grad.reshape(row_size, -1, half_grad.shape[1]))
@@ -988,12 +1228,22 @@
         grad_shift_two,
         grad_force,
     )
-    if covers:
+    if dealt:
         flat = jnp.concatenate([x.reshape(-1) for x in small])
         devices = row_size * lax.axis_size("wt")
         piece = -(-flat.shape[0] // (devices * 8 * 128)) * 128
         flat = jnp.pad(flat, (0, devices * 8 * piece - flat.shape[0]))
-        flat = total_over_all(flat.reshape(devices, 8, piece)).reshape(-1)
+        flat, atoms_grad, out_low, forces_in = total_over_all(
+            flat.reshape(devices, 8, piece),
+            quarters(atoms_grad),
+            quarters(out_low),
+            jnp.pad(force_rows, ((0, 5), (0, 0))),
+        )
+        flat = flat.reshape(-1)
+        atoms_grad = atoms_grad.reshape(row_count, model_width)
+        out_low = out_low.reshape(row_count, model_width)
+        forces_in = lax.dynamic_slice_in_dim(forces_in[:, :3, :], outer * QB, QB, 2)
+        force_rows = jnp.swapaxes(forces_in, 0, 1).reshape(3, row_count)
         small_sums, at = [], 0
         for x in small:
             small_sums.append(flat[at : at + x.size].reshape(x.shape))

time: 476 us -> 434 us (0.912)
  Pallas kernels: 205 us -> 309 us
  starting transfers between devices: 118 us -> 35.6 us
  local copies, waits for them, and re-layouts: 58.5 us -> 25.5 us
  matrix products: 43.6 us -> 24.5 us
  waiting for transfers between devices: 10.8 us -> 2.09 us
    ppermute x3, starting transfers between devices: 108 us -> 27.7 us  [to_columns(): arrived.append(lax.ppermute(others[step - 1], 'row', pairs))]
    pallas_call x2, Pallas kernels: 71.2 us -> 127 us  [the longest x1 86.7 us: front(): pl.pallas_call(front_kernel, out_shape=[shape((total, width), f32), shape...]
    pallas_call x1, Pallas kernels: 48.5 us -> 75.3 us  [attention_backward(): pl.pallas_call(functools.partial(bwd_kernel, head_dim), grid_spec=pltpu.P...]
    pallas_call x1, Pallas kernels: 19.1 us -> 38.9 us  [attention_forward(): pl.pallas_call(functools.partial(fwd_kernel, head_dim), grid_spec=pltpu.P...]
    dot_general x4 -> x0, matrix products: 13.3 us -> none  [the longest x1 6.53 us: on_device(): keys = jnp.dot(every, w_k, preferred_element_type=f32).astype(bf16)]
    ppermute x3, waiting for transfers between devices: 9.37 us -> 0.01 us  [to_planes(): lax.ppermute(by_plane(ffn_grads, inner ^ flip), 'row', pairs)]
    reshape x4 -> x1, local copies, waits for them, and re-layouts: 8.6 us -> 0.85 us  [padded(): jnp.pad(split, pads)]
    reshape x2, local copies, waits for them, and re-layouts: 7.3 us -> 0.16 us  [the longest x1 0.08 us: on_device(): flat.reshape(devices, 8, piece)]
  transfers between devices with their start and end apart: 16 -> 15, of which waited for: 2 -> 0; matrix products, arithmetic and copies ran while one was open for 18% -> 10% of each run, Pallas kernels for 38% -> 62%
where the time goes in v3:
time: 434 us; the launch traced here: 430 us
  Pallas kernels  309 us (71%)
  starting transfers between devices  35.6 us (8%)
  local copies, waits for them, and re-layouts  25.5 us (6%)
  matrix products  24.5 us (6%)
  other arithmetic  18.5 us (4%)
  between operations  15.3 us (4%)
    pallas_call x1, Pallas kernels, front(): pl.pallas_call(front_kernel, out_shape=[shape((total, width), f32), shape...  86.7 us
    pallas_call x1, Pallas kernels, attention_backward(): pl.pallas_call(functools.partial(bwd_kernel, head_dim), grid_spec=pltpu.P...  75.3 us
    pallas_call x1, Pallas kernels, finish_rows(): pl.pallas_call(functools.partial(finish_kernel, outers, head_dim), out_sh...  67.6 us
    pallas_call x1, Pallas kernels, total_over_all(): pl.pallas_call(functools.partial(total_kernel, count), out_shape=[shape(x...  40.3 us
    pallas_call x1, Pallas kernels, attention_forward(): pl.pallas_call(functools.partial(fwd_kernel, head_dim), grid_spec=pltpu.P...  38.9 us
    ppermute x3, starting transfers between devices, to_columns(): arrived.append(lax.ppermute(others[step - 1], 'row', pairs))  27.7 us
    dot_general x4, matrix products, along_rows(): lax.dot_general(left_side, right_side, (((1,), (1,)), ((), ())), preferre...  10.9 us
  transfers between devices with their start and end apart: 15, of which 0 were waited for; matrix products, arithmetic and copies ran while one was open for 10% of the time, Pallas kernels for 62%

profile of v3, /device:TPU:0, one launch (start us, length us, event | category | flops | bytes accessed | tf_op | source)
XLA Modules:
  0.0 430.4 jit_solution(16400575791657968821)
XLA Ops:
  14.3 86.7 %front.1 = (f32[128,768]{1,0:T(8,128)}, bf16[4,32,768]{2,1,0:T(8,128)(2,1)}, f32[4,8,128]{2,1,0:T(8,128)}, bf16[4,16,32,768]{3,2,1,0:T(8,128)(2,1)}, bf16[16,16,...) custom-call(bf16[4,32,768]{2,1,0:T(8,128)(2,1)} %bitcast.113, ...), custom_call_target="tpu_custom_call" | custom-call | tf_op jit(solution)/shard_map/front/pallas_call | solution.py:615
  101.0 1.4 slice_convert_fusion
  107.5 38.9 %attend.1 = (bf16[4,16,1024,128]{3,2,1,0:T(8,128)(2,1)}, f32[128,1024]{1,0:T(8,128)}, f32[4096,128]{1,0:T(8,128)}) custom-call(s32[4]{0:T(128)} %get-tuple-element.177.lo_ref, s32[4]{0:T(128)} %get-tuple-element.176.hi_ref, bf16[128,1024]{1,0:T(8,128)(2,1)} %get-tuple-element.59.q_ref, bf16[16,1024,128]{2,1,0:T(8,128)(2,1)} %get-tuple-element.60.kt_ref, ...), custom_call_target="tpu_custom_call" | custom-call | flops 30000001024 | bytes 40000000 | tf_op jit(solution)/shard_map/attend/pallas_call | solution.py:291
  146.4 1.1 convert.6
  150.8 0.8 add_convert_fusion.own_ref
  151.7 1.7 fusion.54
  154.5 4.7 %multiply_convert_fusion = (bf16[128,3072]{1,0:T(8,128)(2,1)S(1)}, f32[128,3072]{1,0:T(8,128)}) fusion(bf16[128,768]{1,0:T(8,128)(2,1)S(1)} %add_convert_fusion.1, bf16[768,3072]{1,0:T(8,128)(2,1)} %all-gather.6.cloned.1.call-done), kind=kOutput, calls=%fused_computation.19 | convolution fusion | flops 607518720 | bytes 7274496 | tf_op jit(solution)/shard_map/dot_general | solution.py:1071
  159.1 6.2 %fusion.6 = bf16[128,3072]{1,0:T(8,128)(2,1)} fusion(f32[128,3072]{1,0:T(8,128)} %get-tuple-element.175, bf16[128,768]{1,0:T(8,128)(2,1)S(1)} %get-tuple-element.171, bf16[3072,768]{1,0:T(8,128)(2,1)} %all-gather.8.cloned.1.call-done), kind=kOutput, calls=%fused_computation.13 | convolution fusion | flops 614203392 | bytes 7274496 | tf_op jit(solution)/shard_map/dot_general | solution.py:79
  165.3 3.1 multiply_reduce_fusion
  168.5 0.9 fusion.49
  169.8 0.8 broadcast_select_fusion
  170.6 0.8 fusion.12
  171.9 1.5 convolution_convert_fusion.7
  173.6 0.9 copy.75.do_ref
  174.6 1.5 convolution_convert_fusion.6
  177.8 2.4 convolution_convert_fusion
  181.0 2.4 dynamic-slice_bitcast_fusion
  183.4 1.1 copy-done.2
  184.4 5.0 %collective-permute-start.7 = (bf16[4,432,384]{2,1,0:T(8,128)(2,1)}, bf16[4,432,384]{2,1,0:T(8,128)(2,1)}, u32[]{:S(2)}, u32[]{:S(2)}) collective-permute-start(bf16[4,432,384]{2,1,0:T(8,128)(2,1)} %get-tuple-element.141), channel_id=1, source_target_pairs={{0,4},{2,6},{4,0},{6,2},{8,12},{10,14},{12,8},{14,10},{16,20},{18,... | collective-permute-start | bytes 3981320 | tf_op jit(solution)/shard_map/ppermute | solution.py:1140
  189.5 1.5 collective-permute-start.8
  190.9 75.3 %attend_back.1 = (bf16[128,1024]{1,0:T(8,128)(2,1)}, bf16[768,2048]{1,0:T(8,128)(2,1)}, bf16[768,2048]{1,0:T(8,128)(2,1)}, f32[32,128]{1,0:T(8,128)}, f32[3,128,128]{2,1,0:T(8,128)}) custom-call(s32[4]{0:T(128)} %get-tuple-element.177.lo_ref, s32[4]{0:T(128)} %get-tuple-element.176.hi_ref, bf16[4,16,1024,128]{3,2,1,0:T(8,128)(2,1)} %get-tuple-element.64.p_ref, ...), custom_call_target="tpu_custom_call" | custom-call | flops 60000002048 | bytes 60000000 | tf_op jit(solution)/shard_map/attend_back/pallas_call | solution.py:348
  266.3 3.1 fusion.2
  269.5 1.6 copy-done.3
  271.3 27.7 %collective-permute-start.10 = (bf16[432,384]{1,0:T(8,128)(2,1)S(1)}, bf16[432,384]{1,0:T(8,128)(2,1)S(1)}, u32[]{:S(2)}, u32[]{:S(2)}) collective-permute-start(bf16[432,384]{1,0:T(8,128)(2,1)S(1)} %get-tuple-element.83), channel_id=1, source_target_pairs={{0,16},{2,18},{4,20},{6,22},{8,24},{10,26},{12,28},{14,30},{16,0},... | collective-permute-start | bytes 995336 | tf_op jit(solution)/shard_map/ppermute | solution.py:1160
  299.3 1.1 reduce_sum.160
  300.6 67.6 %finish_rows.1 = (f32[128,768]{1,0:T(8,128)}, f32[144,384]{1,0:T(8,128)}) custom-call(bf16[768,2048]{1,0:T(8,128)(2,1)} %get-tuple-element.69.dkt_ref, bf16[768,2048]{1,0:T(8,128)(2,1)} %get-tuple-element.70.dvt_ref, bf16[128,1024]{1,0:T(8,128)(2,1)} %get-tuple-element.77.dq_ref, bf16[2048,768]{1,0:T(8,128)(2,1)} %bitcast.97, ...), custom_call_target="tpu_custom_call" | custom-call | tf_op jit(solution)/shard_map/finish_rows/pallas_call | solution.py:773
  368.3 1.5 multiply_reduce_fusion.1
  369.8 1.2 multiply_add_fusion.2
  371.9 40.3 %total_over_all.1 = (f32[32,8,512]{2,1,0:T(8,128)S(1)}, f32[4,32,768]{2,1,0:T(8,128)S(1)}, bf16[4,32,768]{2,1,0:T(8,128)(2,1)S(1)}, f32[4,8,128]{2,1,0:T(8,128)S(1)}) custom-call(f32[32,8,512]{2,1,0:T(8,128)S(1)} %reshape.294.x_ref, f32[4,32,768]{2,1,0:T(8,128)S(1)} %bitcast.90, bf16[4,32,768]{2,1,0:T(8,128)(2,1)S(1)} %bitcast.91, f32[8,128]{1,0:T(8,128)S(1)} %pad.19.fo_ref), custom_call_target="tpu_custom_call" | custom-call | tf_op jit(solution)/shard_map/total_over_all/pallas_call | solution.py:894
  413.6 1.9 slice.138
  415.4 1.3 bitcast_add_fusion
  418.9 0.8 reshape.297
  (200 shorter events, 28.4 us)
Async XLA Ops:
  7.2 141.5 %copy-start = (bf16[3,768]{1,0:T(4,128)(2,1)S(1)}, bf16[3,768]{1,0:T(4,128)(2,1)}, u32[]{:S(2)}) copy-start(bf16[3,768]{1,0:T(4,128)(2,1)} %param.37) | copy-start | bytes 13828
  7.2 144.5 %all-gather.4.cloned.1.call-start = ((), (), s32[]{:S(2)}) async-start(), calls=%async_computation | async-start | bytes 1769472 | tf_op jit(solution)/shard_map/all_gather | solution.py:979
  7.9 146.5 %all-gather.6.cloned.1.call-start = ((), (), s32[]{:S(2)}) async-start(), calls=%async_computation.1 | async-start | bytes 7077888 | tf_op jit(solution)/shard_map/all_gather | solution.py:980
  8.7 3.3 copy-start.16
  8.7 3.8 copy-start.18
  8.7 5.0 %copy-start.24 = (bf16[3,1,128]{2,0,1:T(4,128)(2,1)S(1)}, bf16[3,1,128]{2,0,1:T(4,128)(2,1)}, u32[]{:S(2)}) copy-start(bf16[3,1,128]{2,0,1:T(4,128)(2,1)} %param.21) | copy-start | bytes 2308
  8.7 150.4 %all-gather.8.cloned.1.call-start = ((), (), s32[]{:S(2)}) async-start(), calls=%async_computation.2 | async-start | bytes 7077888 | tf_op jit(solution)/shard_map/all_gather | solution.py:981
  10.3 94.3 %copy-start.27 = (f32[128]{0:T(128)S(1)}, f32[128]{0:T(128)}, u32[]{:S(2)}) copy-start(f32[128]{0:T(128)} %param.30) | copy-start | bytes 1540
  10.4 94.9 %copy-start.25 = (f32[128]{0:T(128)S(1)}, f32[128]{0:T(128)}, u32[]{:S(2)}) copy-start(f32[128]{0:T(128)} %param.29) | copy-start | bytes 1540
  147.5 2.9 copy-start.1
  148.7 25.7 %collective-permute-start.3 = (bf16[128,384]{1,0:T(8,128)(2,1)}, bf16[128,384]{1,0:T(8,128)(2,1)}, u32[]{:S(2)}, u32[]{:S(2)}) collective-permute-start(bf16[128,384]{1,0:T(8,128)(2,1)} %get-tuple-element.160), channel_id=1, source_target_pairs={{0,1},{1,0},{2,3},{3,2},{4,5},{5,4},{6,7},{7,6},{8,9},{9,8},{10,11... | collective-permute-start | bytes 294920 | tf_op jit(solution)/shard_map/ppermute | solution.py:30
  149.1 26.9 %collective-permute-start.4 = (bf16[128,768]{1,0:T(8,128)(2,1)S(1)}, bf16[128,768]{1,0:T(8,128)(2,1)S(1)}, u32[]{:S(2)}, u32[]{:S(2)}) collective-permute-start(bf16[128,768]{1,0:T(8,128)(2,1)S(1)} %get-tuple-element.171), channel_id=1, source_target_pairs={{0,1},{1,0},{2,3},{3,2},{4,5},{5,4},{6,7},{7,6},{8,9},{9,8},{10,11... | collective-permute-start | bytes 589832 | tf_op jit(solution)/shard_map/ppermute | solution.py:30
  150.8 2.8 copy-start.17
  159.1 6.2 %copy-start.5 = (bf16[768,3072]{1,0:T(8,128)(2,1)S(1)}, bf16[768,3072]{1,0:T(8,128)(2,1)}, u32[]{:S(2)}) copy-start(bf16[768,3072]{1,0:T(8,128)(2,1)} %all-gather.6.cloned.1.call-done) | copy-start | bytes 14155780
  165.3 12.4 %collective-permute-start = (bf16[128,3072]{1,0:T(8,128)(2,1)}, bf16[128,3072]{1,0:T(8,128)(2,1)}, u32[]{:S(2)}, u32[]{:S(2)}) collective-permute-start(bf16[128,3072]{1,0:T(8,128)(2,1)} %fusion.6), channel_id=1, source_target_pairs={{0,1},{1,0},{2,3},{3,2},{4,5},{5,4},{6,7},{7,6},{8,9},{9,8},{10,11... | collective-permute-start | bytes 2359304 | tf_op jit(solution)/shard_map/ppermute | solution.py:30
  165.3 5.3 %copy-start.4 = (bf16[3072,768]{1,0:T(8,128)(2,1)S(1)}, bf16[3072,768]{1,0:T(8,128)(2,1)}, u32[]{:S(2)}) copy-start(bf16[3072,768]{1,0:T(8,128)(2,1)} %all-gather.8.cloned.1.call-done) | copy-start | bytes 14155780
  169.3 5.2 %collective-permute-start.2 = (bf16[128,768]{1,0:T(8,128)(2,1)}, bf16[128,768]{1,0:T(8,128)(2,1)}, u32[]{:S(2)}, u32[]{:S(2)}) collective-permute-start(bf16[128,768]{1,0:T(8,128)(2,1)} %get-tuple-element.138), channel_id=1, source_target_pairs={{0,1},{1,0},{2,3},{3,2},{4,5},{5,4},{6,7},{7,6},{8,9},{9,8},{10,11... | collective-permute-start | bytes 589832 | tf_op jit(solution)/shard_map/ppermute | solution.py:30
  170.6 5.5 %collective-permute-start.5 = (bf16[128,1536]{1,0:T(8,128)(2,1)}, bf16[128,1536]{1,0:T(8,128)(2,1)S(1)}, u32[]{:S(2)}, u32[]{:S(2)}) collective-permute-start(bf16[128,1536]{1,0:T(8,128)(2,1)} %get-tuple-element.146), channel_id=1, source_target_pairs={{0,1},{1,0},{2,3},{3,2},{4,5},{5,4},{6,7},{7,6},{8,9},{9,8},{10,11... | collective-permute-start | bytes 1179656 | tf_op jit(solution)/shard_map/ppermute | solution.py:30
  174.4 3.2 collective-permute-start.1
  180.9 3.5 copy-start.2
  184.4 81.9 %collective-permute-start.6 = (bf16[4,432,384]{2,1,0:T(8,128)(2,1)}, bf16[4,432,384]{2,1,0:T(8,128)(2,1)}, u32[]{:S(2)}, u32[]{:S(2)}) collective-permute-start(bf16[4,432,384]{2,1,0:T(8,128)(2,1)} %get-tuple-element.142), channel_id=1, source_target_pairs={{0,2},{2,0},{4,6},{6,4},{8,10},{10,8},{12,14},{14,12},{16,18},{18,... | collective-permute-start | bytes 3981320 | tf_op jit(solution)/shard_map/ppermute | solution.py:1140
  184.4 81.9 %collective-permute-start.7 = (bf16[4,432,384]{2,1,0:T(8,128)(2,1)}, bf16[4,432,384]{2,1,0:T(8,128)(2,1)}, u32[]{:S(2)}, u32[]{:S(2)}) collective-permute-start(bf16[4,432,384]{2,1,0:T(8,128)(2,1)} %get-tuple-element.141), channel_id=1, source_target_pairs={{0,4},{2,6},{4,0},{6,2},{8,12},{10,14},{12,8},{14,10},{16,20},{18,... | collective-permute-start | bytes 3981320 | tf_op jit(solution)/shard_map/ppermute | solution.py:1140
  189.5 76.8 %collective-permute-start.8 = (bf16[4,432,384]{2,1,0:T(8,128)(2,1)}, bf16[4,432,384]{2,1,0:T(8,128)(2,1)}, u32[]{:S(2)}, u32[]{:S(2)}) collective-permute-start(bf16[4,432,384]{2,1,0:T(8,128)(2,1)} %get-tuple-element.140), channel_id=1, source_target_pairs={{0,6},{2,4},{4,2},{6,0},{8,14},{10,12},{12,10},{14,8},{16,22},{18,... | collective-permute-start | bytes 3981320 | tf_op jit(solution)/shard_map/ppermute | solution.py:1140
  271.0 29.4 %copy-start.19 = (f32[32,128]{1,0:T(8,128)S(1)}, f32[32,128]{1,0:T(8,128)}, u32[]{:S(2)}) copy-start(f32[32,128]{1,0:T(8,128)} %get-tuple-element.87) | copy-start | bytes 49156
  271.2 97.1 %collective-permute-start.9 = (bf16[432,384]{1,0:T(8,128)(2,1)S(1)}, bf16[432,384]{1,0:T(8,128)(2,1)S(1)}, u32[]{:S(2)}, u32[]{:S(2)}) collective-permute-start(bf16[432,384]{1,0:T(8,128)(2,1)S(1)} %get-tuple-element.82), channel_id=1, source_target_pairs={{0,8},{2,10},{4,12},{6,14},{8,16},{10,18},{12,20},{14,22},{16,24},... | collective-permute-start | bytes 995336 | tf_op jit(solution)/shard_map/ppermute | solution.py:1160
  271.3 97.0 %collective-permute-start.10 = (bf16[432,384]{1,0:T(8,128)(2,1)S(1)}, bf16[432,384]{1,0:T(8,128)(2,1)S(1)}, u32[]{:S(2)}, u32[]{:S(2)}) collective-permute-start(bf16[432,384]{1,0:T(8,128)(2,1)S(1)} %get-tuple-element.83), channel_id=1, source_target_pairs={{0,16},{2,18},{4,20},{6,22},{8,24},{10,26},{12,28},{14,30},{16,0},... | collective-permute-start | bytes 995336 | tf_op jit(solution)/shard_map/ppermute | solution.py:1160
  298.9 69.4 %collective-permute-start.11 = (bf16[432,384]{1,0:T(8,128)(2,1)S(1)}, bf16[432,384]{1,0:T(8,128)(2,1)S(1)}, u32[]{:S(2)}, u32[]{:S(2)}) collective-permute-start(bf16[432,384]{1,0:T(8,128)(2,1)S(1)} %get-tuple-element.84), channel_id=1, source_target_pairs={{0,24},{2,26},{4,28},{6,30},{8,0},{10,2},{12,4},{14,6},{16,8},{18,... | collective-permute-start | bytes 995336 | tf_op jit(solution)/shard_map/ppermute | solution.py:1160
  368.3 3.2 copy-start.7
  412.4 3.0 copy-start.8
  412.4 3.0 copy-start.10
  416.7 3.0 slice-start
  418.1 5.0 %copy-start.11 = (f32[144,384]{1,0:T(8,128)S(1)}, f32[144,384]{1,0:T(8,128)}, u32[]{:S(2)}) copy-start(f32[144,384]{1,0:T(8,128)} %get-tuple-element.92) | copy-start | bytes 663556
  (14 other events, 24.9 us)
Sparse Core Ops, SparseCore 0:
  9.6 11.9 all-gather.3
  23.1 16.7 all-gather.5
  41.4 15.6 all-gather.7
